TPU v7x, 256 devices: a whole 4x4x8 slice. The times are simulated.
256 devices in a mesh: tm: 4 (over y), det: 64 (over z, x, core).
Axes of the slice: x: 4, y: 4, z: 8, core: 2. Of those that a mesh axis runs over, the one named last changes fastest.
Arguments:
- offset_amplitude_array: float32 [128, 16], P('det', 'tm'), may hold values from -6 to 6
- system_remainder: float32 [128, 16], P('det', 'tm'), may hold values from -6 to 6
- conjugate_heading: float32 [128, 16], P('det', 'tm'), may hold values from -6 to 6
- region_cell_numbers: int32 [128, 16384], P('det', 'tm'), may hold values from 0 to 255
- stokes_reading_rotation: float32 [128, 16384], P('det', 'tm'), may hold values from -3.140625 to 3.140625
- scan_patch_places: int32 [128, 128], P('det', 'tm'), may hold values from 0 to 127
- holder_visited_regions: int32 [4, 64, 64, 2], P('tm', 'det'), may hold values from 0 to 47, as said below
- stokes_precision_matrices: float32 [3072, 6, 256], P('det'), as said below
Outputs:
- refreshed_offset_amplitudes: float32 [128, 16], P('det', 'tm')
- updated_residual_vector: float32 [128, 16], P('det', 'tm')
- updated_search_direction: float32 [128, 16], P('det', 'tm')
Inputs may be any that keep to these rules, and one draw needn't show every extreme that they name: For each device (i, j) and owner o, holder_visited_regions[i, j, o, :] holds 2 distinct local submaps. `stokes_precision_matrices`: each pixel's 3x3 block is symmetric positive definite.
All inputs are finite; a program needn't handle non-finite values.
Results may differ from a plain program's by a relative error of at most 0.00005.
Values sent between devices are 32-bit elements; how exact they have to be, the bound alone decides.
No kernel may reach another device: no remote copies, remote signals or barrier semaphores. Data moves between devices by JAX's collectives and lax.ppermute only.
A program may use at most 64 MiB of HBM per device.

v0:
```python
import jax
import jax.numpy as jnp
from jax import lax
from jax.sharding import PartitionSpec as P

TILE = 128
WINDOW = 256


stiffness = 0.5


def extended(value, sides, width):
    for axis, dim in sides:
        peers, length = (lax.axis_size(axis), value.shape[dim])
        up = [(i, (i + 1) % peers) for i in range(peers - 1)]
        down = [(j, i) for i, j in up]
        last = lax.slice_in_dim(value, length - width, length, axis=dim)
        leading = lax.slice_in_dim(value, 0, width, axis=dim)
        before = lax.ppermute(last, axis, up)
        after = lax.ppermute(leading, axis, down)
        value = jnp.concatenate([before, value, after], axis=dim)
    return value


def solve_blocks(binned, stokes_precision_matrices):
    first = binned[:, 0]
    second = binned[:, 1]
    third = binned[:, 2]
    out_first = (
        stokes_precision_matrices[:, 0] * first
        + stokes_precision_matrices[:, 1] * second
        + stokes_precision_matrices[:, 2] * third
    )
    out_second = (
        stokes_precision_matrices[:, 1] * first
        + stokes_precision_matrices[:, 3] * second
        + stokes_precision_matrices[:, 4] * third
    )
    out_third = (
        stokes_precision_matrices[:, 2] * first
        + stokes_precision_matrices[:, 4] * second
        + stokes_precision_matrices[:, 5] * third
    )
    return jnp.stack([out_first, out_second, out_third], axis=1)


def shards(
    offset_amplitude_array,
    system_remainder,
    conjugate_heading,
    region_cell_numbers,
    stokes_reading_rotation,
    scan_patch_places,
    holder_visited_regions,
    stokes_precision_matrices,
):
    det_dev, base_dev = conjugate_heading.shape
    samp_dev = region_cell_numbers.shape[1]
    per_owner = holder_visited_regions.shape[3]
    owners = lax.axis_size("det")
    slot_count = owners * per_owner
    sub_dev = stokes_precision_matrices.shape[0]
    cells = 3 * WINDOW
    stream = jnp.repeat(conjugate_heading, samp_dev // base_dev, axis=1)
    twice = 2.0 * stokes_reading_rotation
    cos_weight = jnp.cos(twice)
    sin_weight = jnp.sin(twice)
    slot_index = jnp.repeat(scan_patch_places, TILE, axis=1)
    cell = slot_index * cells + region_cell_numbers
    values = jnp.concatenate(
        [stream.ravel(), (stream * cos_weight).ravel(), (stream * sin_weight).ravel()]
    )
    targets = jnp.concatenate([cell.ravel(), (cell + WINDOW).ravel(), (cell + 2 * WINDOW).ravel()])
    local_bins = jax.ops.segment_sum(values, targets, num_segments=slot_count * cells).reshape(
        slot_count, cells
    )
    my_hits = holder_visited_regions.reshape(owners, per_owner)
    global_ids = jnp.arange(slot_count, dtype=jnp.int32) // per_owner * sub_dev + my_hits.reshape(
        -1
    )
    selector = (
        global_ids[None, :] == jnp.arange(sub_dev * owners, dtype=jnp.int32)[:, None]
    ).astype(jnp.float32)
    full_bins = jnp.dot(
        selector, local_bins, precision=lax.Precision.HIGHEST, preferred_element_type=jnp.float32
    )
    owned = lax.psum_scatter(full_bins, "det", scatter_dimension=0, tiled=True)
    binned = lax.psum(owned, "tm")
    sky_map = solve_blocks(binned.reshape(sub_dev, 3, WINDOW), stokes_precision_matrices).reshape(
        sub_dev, cells
    )
    whole_sky = lax.all_gather(sky_map, "det", axis=0, tiled=True)
    slot_sky = jnp.dot(
        selector.T, whole_sky, precision=lax.Precision.HIGHEST, preferred_element_type=jnp.float32
    )
    flat_sky = slot_sky.reshape(-1)
    scanned = (
        flat_sky[cell]
        + cos_weight * flat_sky[cell + WINDOW]
        + sin_weight * flat_sky[cell + 2 * WINDOW]
    )
    folded = scanned.reshape(det_dev, base_dev, samp_dev // base_dev).sum(axis=2) / (
        samp_dev // base_dev
    )
    padded = extended(conjugate_heading, (("tm", 1),), 1)
    applied = (
        conjugate_heading
        + folded
        + stiffness * (2.0 * conjugate_heading - padded[:, :-2] - padded[:, 2:])
    )
    norm_now, curvature = lax.psum(
        (jnp.sum(system_remainder * system_remainder), jnp.sum(conjugate_heading * applied)),
        ("tm", "det"),
    )
    conjugate_update_factor = norm_now / curvature
    updated_residual_vector = system_remainder - conjugate_update_factor * applied
    norm_next = lax.psum(jnp.sum(updated_residual_vector * updated_residual_vector), ("tm", "det"))
    refreshed_offset_amplitudes = (
        offset_amplitude_array + conjugate_update_factor * conjugate_heading
    )
    updated_search_direction = updated_residual_vector + norm_next / norm_now * conjugate_heading
    return (refreshed_offset_amplitudes, updated_residual_vector, updated_search_direction)


def solution(mesh):
    return jax.shard_map(
        shards,
        mesh=mesh,
        in_specs=(
            P("det", "tm"),
            P("det", "tm"),
            P("det", "tm"),
            P("det", "tm"),
            P("det", "tm"),
            P("det", "tm"),
            P("tm", "det", None, None),
            P("det", None, None),
        ),
        out_specs=(P("det", "tm"), P("det", "tm"), P("det", "tm")),
        check_vma=False,
    )
```

profile of v0, /device:TPU:1, one launch (start us, length us, event | category | flops | bytes accessed | tf_op | source)
XLA Modules:
  0.0 786.2 jit_solution(1612959436937574905)
XLA Ops:
  7.2 0.0 reduce-scatter.2.cloned.1.call-start
  7.2 0.7 broadcast_multiply_fusion
  7.9 0.1 broadcast_bitcast_fusion.2
  8.0 0.8 fusion.12
  8.9 0.8 broadcast_bitcast_fusion.1
  9.7 1.2 multiply_bitcast_fusion.1
  11.0 169.6 %scatter_custom_fusion = f32[98304]{0:T(1024)S(1)} fusion(s32[24576]{0:T(1024)S(1)} %pad_add_fusion, f32[24576]{0:T(1024)S(1)} %pad_maximum_fusion.1, f32[]{:T(128)} %constant.14.clone.1), kind=kCustom, calls=%fused_computation.10 | custom fusion | flops 24576 | bytes 393220 | tf_op jit(solution)/shard_map/scatter-add | solution.py:75
  180.6 0.1 reshape.67
  180.7 0.8 copy.13
  181.4 0.1 reshape_reshape.6
  181.6 0.0 copy-start
  181.6 6.2 fusion.1
  187.8 0.0 reduce-scatter.2.cloned.1.call-update
  187.8 0.0 all-reduce.3.cloned.1.call-start
  187.9 154.9 %reduce-scatter.2.cloned.1.call-done = f32[48,768]{1,0:T(8,128)} async-done(((f32[3072,768]{1,0:T(8,128)}), f32[48,768]{1,0:T(8,128)}) %reduce-scatter.2.cloned.1.call-update) | async-done | bytes 147472 | tf_op jit(solution)/shard_map/reduce_scatter | solution.py:88
  342.8 1.6 reshape.68
  344.5 0.0 all-reduce.3.cloned.1.call-update
  344.5 0.0 all-gather.2.cloned.1.call-start
  344.5 0.0 copy-done
  344.6 47.9 %all-reduce.3.cloned.1.call-done = f32[48,3,256]{2,1,0:T(4,128)} async-done(((f32[48,3,256]{2,1,0:T(4,128)}), f32[48,3,256]{2,1,0:T(4,128)}) %all-reduce.3.cloned.1.call-update) | async-done | bytes 147472 | tf_op jit(solution)/shard_map/psum | solution.py:89
  392.5 1.4 fusion.10
  393.9 0.1 pad_maximum_fusion
  394.1 0.7 copy.31
  394.7 0.0 all-gather.2.cloned.1.call-update
  394.8 0.0 copy-done.2
  394.8 0.1 fusion.17
  394.9 2.2 collective-permute-start
  397.1 1.3 collective-permute-start.1
  398.5 0.0 collective-permute-done
  398.5 3.0 collective-permute-done.1
  401.5 0.1 pad_maximum_fusion.2
  401.5 80.8 %all-gather.2.cloned.1.call-done = f32[3072,768]{1,0:T(8,128)} async-done(((f32[48,768]{1,0:T(8,128)}), f32[3072,768]{1,0:T(8,128)}) %all-gather.2.cloned.1.call-update) | async-done | bytes 9437200 | tf_op jit(solution)/shard_map/all_gather | solution.py:93
  482.3 7.3 fusion
  489.7 45.5 %gather_fusion = f32[8192]{0:T(1024)S(1)} fusion(f32[98304]{0:T(1024)S(1)} %reshape.70, s32[8192]{0:T(1024)S(1)} %broadcast_clamp_fusion.2), kind=kCustom, calls=%fused_computation | custom fusion | bytes 98304 | tf_op jit(solution)/shard_map/gather | solution.py:99
  535.3 45.5 %gather_fusion.1 = f32[8192]{0:T(1024)S(1)} fusion(f32[98304]{0:T(1024)S(1)} %reshape.70, s32[8192]{0:T(1024)S(1)} %broadcast_clamp_fusion.1), kind=kCustom, calls=%fused_computation.1 | custom fusion | bytes 98304 | tf_op jit(solution)/shard_map/gather | solution.py:100
  580.9 0.0 copy-start.1
  580.9 0.0 copy-start.3
  580.9 0.0 copy-start.5
  580.9 45.5 %gather_fusion.2 = f32[8192]{0:T(1024)S(1)} fusion(f32[98304]{0:T(1024)S(1)} %reshape.70, s32[8192]{0:T(1024)S(1)} %broadcast_clamp_fusion), kind=kCustom, calls=%fused_computation.2 | custom fusion | bytes 98304 | tf_op jit(solution)/shard_map/gather | solution.py:101
  626.5 0.0 copy-done.1
  626.5 0.5 multiply_add_fusion
  627.0 0.1 reduce_sum.37
  627.1 0.7 multiply_reduce_fusion.1
  627.8 74.6 %all-reduce = (f32[]{:T(128)}, f32[]{:T(128)}) all-reduce(f32[]{:T(128)} %get-tuple-element.34, f32[]{:T(128)} %get-tuple-element.7), channel_id=1, replica_groups=mesh['tm'=4,'det'=64] {'tm','det'}, use_global_device_ids=true, to_apply=%region_1.2 | all-reduce | flops 2 | bytes 16 | tf_op jit(solution)/shard_map/psum | solution.py:112
  703.8 0.6 multiply_reduce_fusion
  704.4 73.4 %psum.31 = f32[]{:T(128)} all-reduce(f32[]{:T(128)} %get-tuple-element.5), channel_id=1, replica_groups=mesh['tm'=4,'det'=64] {'tm','det'}, use_global_device_ids=true, to_apply=%region_9.10 | all-reduce | flops 1 | bytes 8 | tf_op jit(solution)/shard_map/psum | solution.py:118
  779.1 0.6 multiply_add_fusion.1
  779.7 0.0 copy-done.4
  (27 shorter events, 0.3 us)
Async XLA Ops:
  7.2 335.6 %reduce-scatter.2.cloned.1.call-start = ((), (), s32[]{:S(2)}) async-start(), calls=%async_computation.1 | async-start | bytes 9584640 | tf_op jit(solution)/shard_map/reduce_scatter | solution.py:88
  181.6 163.0 %copy-start = (f32[48,6,256]{2,0,1:T(8,128)S(1)}, f32[48,6,256]{2,0,1:T(8,128)}, u32[]{:S(2)}) copy-start(f32[48,6,256]{2,0,1:T(8,128)} %param.15) | copy-start | bytes 884740
  187.8 207.0 %copy-start.2 = (f32[2,4]{1,0:T(2,128)S(1)}, f32[2,4]{1,0:T(2,128)}, u32[]{:S(2)}) copy-start(f32[2,4]{1,0:T(2,128)} %param.10) | copy-start | bytes 100
  187.8 204.7 %all-reduce.3.cloned.1.call-start = ((), (), s32[]{:S(2)}) async-start(), calls=%async_computation.2 | async-start | bytes 393216 | tf_op jit(solution)/shard_map/psum | solution.py:89
  344.5 137.9 %all-gather.2.cloned.1.call-start = ((), (), s32[]{:S(2)}) async-start(), calls=%async_computation.3 | async-start | bytes 9584640 | tf_op jit(solution)/shard_map/all_gather | solution.py:93
  394.9 3.6 collective-permute-start
  397.1 4.4 collective-permute-start.1
  580.9 45.6 %copy-start.1 = (f32[2,4096]{1,0:T(2,128)S(1)}, f32[2,4096]{1,0:T(2,128)}, u32[]{:S(2)}) copy-start(f32[2,4096]{1,0:T(2,128)} %param.12) | copy-start | bytes 98308
  580.9 46.2 %copy-start.3 = (f32[2,4]{1,0:T(2,128)S(1)}, f32[2,4]{1,0:T(2,128)}, u32[]{:S(2)}) copy-start(f32[2,4]{1,0:T(2,128)} %param.9) | copy-start | bytes 100
  580.9 198.2 %copy-start.5 = (f32[2,4]{1,0:T(2,128)S(1)}, f32[2,4]{1,0:T(2,128)}, u32[]{:S(2)}) copy-start(f32[2,4]{1,0:T(2,128)} %param.8) | copy-start | bytes 100
  704.4 75.3 %copy-start.4 = (f32[2,4]{1,0:T(2,128)}, f32[2,4]{1,0:T(2,128)S(1)}, u32[]{:S(2)}) copy-start(f32[2,4]{1,0:T(2,128)S(1)} %get-tuple-element.6) | copy-start | bytes 100
Sparse Core Ops, SparseCore 0:
  187.9 154.8 reduce-scatter.1
  345.1 47.3 all-reduce.2
  395.2 87.0 all-gather.1
where the time goes:
time: 787 us; the launch traced here: 786 us
  waiting for transfers between devices  287 us (36%)
  other arithmetic  176 us (22%)
  blocking collectives  148 us (19%)
  local copies, waits for them, and re-layouts  141 us (18%)
  between operations  16.7 us (2%)
  matrix products  13.5 us (2%)
    scatter-add x1, other arithmetic, shards(): jax.ops.segment_sum(values, targets, num_segments=slot_count * cells)  170 us
    reduce_scatter x1, waiting for transfers between devices, shards(): owned = lax.psum_scatter(full_bins, 'det', scatter_dimension=0, tiled=True)  155 us
    all_gather x1, waiting for transfers between devices, shards(): whole_sky = lax.all_gather(sky_map, 'det', axis=0, tiled=True)  80.8 us
    psum x1, blocking collectives, shards(): lax.psum((jnp.sum(system_remainder * system_remainder), jnp.sum(conjugate...  74.6 us
    psum x1, blocking collectives, shards(): lax.psum(jnp.sum(updated_residual_vector * updated_residual_vector), ('tm...  73.4 us
    psum x1, waiting for transfers between devices, shards(): binned = lax.psum(owned, 'tm')  47.9 us
    gather x2, local copies, waits for them, and re-layouts, shards(): flat_sky[cell + 2 * WINDOW]  45.6 us
    gather x2, local copies, waits for them, and re-layouts, shards(): flat_sky[cell] + cos_weight * flat_sky[cell + WINDOW]  45.6 us
  transfers between devices with their start and end apart: 5, of which 4 were waited for; matrix products, arithmetic and copies ran while one was open for 0% of the time, Pallas kernels for 0%

commit v1 on v0

v1 whole, which is shorter than its diff:
```python
import functools

import jax
import jax.numpy as jnp
import numpy as np
from jax import lax
from jax.experimental import pallas as pl
from jax.experimental.pallas import tpu as pltpu
from jax.sharding import PartitionSpec as P

TILE = 128
WINDOW = 256
STIFFNESS = 0.5
BF16 = jnp.bfloat16
F32 = jnp.float32
I32 = jnp.int32
NT = (((1,), (1,)), ((), ()))
NN = (((1,), (0,)), ((), ()))


def iota(shape, dim):
    return lax.broadcasted_iota(I32, shape, dim)


def dot(a, b, dims=NN):
    return lax.dot_general(a, b, dims, preferred_element_type=F32)


def split(x):
    high = x.astype(BF16)
    return high, (x - high.astype(F32)).astype(BF16)


def cos_sin(x):
    n = jnp.floor(x * np.float32(2.0 / np.pi) + 0.5)
    r = x - n * np.float32(1.5703125)
    r = r - n * np.float32(4.837512969970703e-4)
    r = r - n * np.float32(7.549789948768648e-8)
    z = r * r
    s = np.float32(-1.9515295891e-4) * z + np.float32(8.3321608736e-3)
    s = (s * z + np.float32(-1.6666654611e-1)) * z * r + r
    c = np.float32(2.443315711809948e-5) * z + np.float32(-1.388731625493765e-3)
    c = (c * z + np.float32(4.166664568298827e-2)) * z * z - 0.5 * z + 1.0
    q = n.astype(I32)
    odd = (q & 1) == 1
    cosine = jnp.where(odd, s, c)
    sine = jnp.where(odd, c, s)
    cosine = jnp.where(((q + 1) & 2) == 2, -cosine, cosine)
    sine = jnp.where((q & 2) == 2, -sine, sine)
    return cosine, sine


def tile_parts(row, slot, pix_ref, cos_ref, sin_ref):
    hot = iota((WINDOW, TILE), 0) == pix_ref[pl.ds(row, 1), :]
    hot = jnp.where(hot, 1.0, 0.0).astype(BF16)
    sub = iota((8, TILE), 0)
    part = sub & 3
    weight = jnp.where(
        part == 0, 1.0, jnp.where(part == 1, cos_ref[pl.ds(row, 1), :], sin_ref[pl.ds(row, 1), :])
    )
    mine = (sub >> 2) == ((slot >> 1) & 1)
    weight = jnp.where(mine & (part < 3), weight, 0.0)
    return hot, weight


def bin_kernel(slot_ref, dir_ref, pix_ref, ang_ref, hits_ref, out_ref, cos_ref, sin_ref, acc_ref):
    c, s = cos_sin(2.0 * ang_ref[...])
    cos_ref[...] = c
    sin_ref[...] = s
    acc_ref[...] = jnp.zeros_like(acc_ref)
    tiles = pix_ref.shape[0]
    dets, bases = dir_ref.shape
    span = tiles // dets // bases

    def group(g, carry):
        det, base = g % dets, g // dets
        height = dir_ref[det, base]
        for t in range(span):
            tile = base * span + t
            slot = slot_ref[det, tile]
            hot, weight = tile_parts(tile * dets + det, slot, pix_ref, cos_ref, sin_ref)
            high = weight.astype(BF16).astype(F32)
            both = jnp.concatenate([high, weight - high], axis=0).astype(BF16)
            res = dot(both, hot, NT)
            res = (res[:8] + res[8:]) * height
            place = (slot & 1) * (acc_ref.shape[0] // 2) + (slot >> 2)
            acc_ref[place] = acc_ref[place] + res
        return carry

    lax.fori_loop(0, dets * bases, group, 0)

    pairs = acc_ref.shape[0] // 2
    sub = iota((8, TILE), 0)
    left = iota((8, TILE), 1) < 64
    last = (sub & 3) == 3
    hits = jnp.broadcast_to(hits_ref[...], (8, TILE))
    for u in range(pairs):
        for b in range(2):
            first = acc_ref[u, :, b * TILE : (b + 1) * TILE]
            second = acc_ref[pairs + u, :, b * TILE : (b + 1) * TILE]
            even = jnp.where(left, first, pltpu.roll(second, 64, 1))
            odd = jnp.where(left, pltpu.roll(first, 64, 1), second)
            for q, value in ((2 * b, even), (2 * b + 1, odd)):
                at = (q * pairs + u) * 8
                out_ref[at : at + 8, :] = jnp.where(last, hits, value)


def own_kernel(me_ref, in_ref, prec_ref, out_ref):
    me = me_ref[0]
    quarter = me_ref[1]
    sources = in_ref.shape[0] // 4
    subs = prec_ref.shape[1]
    ids = in_ref[pl.ds(3, sources, stride=4), :].astype(BF16)
    lane = iota((16, TILE), 1)
    row = iota((16, TILE), 0)
    pick = jnp.where((lane == me + 64 * row) & (row < 2), 1.0, 0.0).astype(BF16)
    id_rows = dot(pick, ids, NT).astype(I32)
    sub = iota((subs, sources), 0)
    hot = jnp.concatenate(
        [
            jnp.where(sub == id_rows[0:1, :], 1.0, 0.0),
            jnp.where(sub == id_rows[1:2, :], 1.0, 0.0),
        ],
        axis=0,
    ).astype(BF16)
    left = iota((subs, TILE), 1) < 64
    binned = []
    for c in range(3):
        high, low = split(in_ref[pl.ds(c, sources, stride=4), :])
        res = dot(hot, jnp.concatenate([high, low], axis=1))
        res = res[:, :TILE] + res[:, TILE:]
        res = jnp.where(left, res[:subs], res[subs:])
        binned.append(res + pltpu.roll(res, 64, 1))

    block = quarter // 2
    keep = left == ((quarter % 2) == 0)
    prec = []
    for e in range(6):
        value = jnp.where(block == 0, prec_ref[e, :, :TILE], prec_ref[e, :, TILE:])
        value = jnp.where(keep, value, 0.0)
        prec.append(value + pltpu.roll(value, 64, 1))
    sky = [
        prec[0] * binned[0] + prec[1] * binned[1] + prec[2] * binned[2],
        prec[1] * binned[0] + prec[3] * binned[1] + prec[4] * binned[2],
        prec[2] * binned[0] + prec[4] * binned[1] + prec[5] * binned[2],
    ]

    deep, wide = iota((TILE, TILE), 0), iota((TILE, TILE), 1)
    spread = jnp.where(deep == me + (wide & 64), 1.0, 0.0).astype(BF16)
    named = dot(ids, spread).astype(I32)
    back = jnp.where(named == (iota((sources, TILE), 1) & 63), 1.0, 0.0).astype(BF16)
    back = jnp.concatenate([back, back], axis=1)
    gap = jnp.zeros((64 - subs, TILE), F32)
    for c in range(3):
        first = jnp.where(left, sky[c], 0.0)
        second = jnp.where(left, 0.0, sky[c])
        high, low = split(jnp.concatenate([first, gap, second, gap], axis=0))
        out_ref[pl.ds(c, sources, stride=4), :] = dot(back, jnp.concatenate([high, low], axis=0))
    out_ref[pl.ds(3, sources, stride=4), :] = jnp.zeros((sources, TILE), F32)


def scan_kernel(
    slot_ref, dir_ref, res_ref, pix_ref, ang_ref, in_ref, out_ref, cos_ref, sin_ref, sky_ref, sum_ref
):
    c, s = cos_sin(2.0 * ang_ref[...])
    cos_ref[...] = c
    sin_ref[...] = s
    pairs = sky_ref.shape[0] // 2
    left = iota((8, TILE), 1) < 64
    for u in range(pairs):
        for b in range(2):
            at = (2 * b * pairs + u) * 8
            even = in_ref[at : at + 8, :]
            at = ((2 * b + 1) * pairs + u) * 8
            odd = in_ref[at : at + 8, :]
            sky_ref[u, :, b * TILE : (b + 1) * TILE] = jnp.where(left, even, pltpu.roll(odd, 64, 1))
            sky_ref[pairs + u, :, b * TILE : (b + 1) * TILE] = jnp.where(
                left, pltpu.roll(even, 64, 1), odd
            )
    tiles = pix_ref.shape[0]
    dets, bases = dir_ref.shape
    span = tiles // dets // bases

    def group(g, carry):
        det, base = g % dets, g // dets
        total = jnp.zeros((8, TILE), F32)
        for t in range(span):
            tile = base * span + t
            slot = slot_ref[det, tile]
            hot, weight = tile_parts(tile * dets + det, slot, pix_ref, cos_ref, sin_ref)
            place = (slot & 1) * pairs + (slot >> 2)
            value = sky_ref[place]
            high = value.astype(BF16).astype(F32)
            both = jnp.concatenate([high, value - high], axis=0).astype(BF16)
            res = dot(both, hot)
            total = total + (res[:8] + res[8:]) * weight
        sum_ref[pl.ds(det * bases + base, 1), :] = jnp.sum(total, axis=0, keepdims=True)
        return carry

    lax.fori_loop(0, dets * bases, group, 0)
    count = dets * bases
    sums = jnp.sum(sum_ref[...], axis=1, keepdims=True) * np.float32(1.0 / (span * TILE))
    lane, sub = iota((count, TILE), 1), iota((count, TILE), 0)
    row = jnp.sum(jnp.where(lane == sub, sums, 0.0), axis=0, keepdims=True)
    lane = iota((1, TILE), 1)
    for d in range(dets):
        for b in range(bases):
            k = d * bases + b
            row = jnp.where(lane == count + k, dir_ref[d, b], row)
            row = jnp.where(lane == 2 * count + k, res_ref[d, b], row)
    out_ref[...] = jnp.broadcast_to(row, out_ref.shape)


def end_kernel(me_ref, in_ref, amp_ref, amp_out, res_out, dir_out, keep_ref):
    rows = in_ref.shape[0]
    dets, bases = amp_ref.shape
    count = dets * bases
    owners = me_ref[2]
    x = in_ref[...]
    lane = iota((rows, TILE), 1)
    valid = lane < count
    base = lane % bases
    scan = jnp.where(valid, x, 0.0)
    way = jnp.where(valid, pltpu.roll(x, TILE - count, 1), 0.0)
    rest = jnp.where(valid, pltpu.roll(x, TILE - 2 * count, 1), 0.0)
    step = rows // 4
    zero = jnp.zeros((step, TILE), F32)
    from_left = pltpu.roll(jnp.concatenate([zero, way[:-step]], axis=0), TILE - (bases - 1), 1)
    from_right = pltpu.roll(jnp.concatenate([way[step:], zero], axis=0), bases - 1, 1)
    before = jnp.where(base == 0, from_left, pltpu.roll(way, 1, 1))
    after = jnp.where(base == bases - 1, from_right, pltpu.roll(way, TILE - 1, 1))
    applied = scan + way + STIFFNESS * (2.0 * way - before - after)
    applied = jnp.where(valid, applied, 0.0)

    def total(v):
        return jnp.sum(jnp.sum(v, axis=0, keepdims=True), axis=1, keepdims=True)

    now = total(rest * rest)
    factor = now / total(way * applied)
    fresh = rest - factor * applied
    ratio = total(fresh * fresh) / now
    keep_ref[0] = fresh
    keep_ref[1] = way
    mine = me_ref[1] * step + me_ref[0]
    my_fresh = keep_ref[0, pl.ds(mine, 1), :]
    my_way = keep_ref[1, pl.ds(mine, 1), :]
    move = factor * my_way
    turn = my_fresh + ratio * my_way
    for d in range(dets):
        lo, hi = d * bases, (d + 1) * bases
        amp_out[d : d + 1, :] = amp_ref[d : d + 1, :] + move[:, lo:hi]
        res_out[d : d + 1, :] = my_fresh[:, lo:hi]
        dir_out[d : d + 1, :] = turn[:, lo:hi]


SMEM = pl.BlockSpec(memory_space=pltpu.SMEM)
VMEM = pl.BlockSpec(memory_space=pltpu.VMEM)
AXES = ("tm", "det")


def exchange(value, rows):
    peers = value.shape[0] // rows
    moved = lax.all_to_all(value.reshape(peers, rows, TILE), AXES, 0, 0, tiled=True)
    return moved.reshape(value.shape)


def shards(amp, res, way, pix, ang, places, hits, prec):
    dets, samples = pix.shape
    per_det = samples // TILE
    tiles = dets * per_det
    owners = hits.shape[2]
    slots = owners * hits.shape[3]
    peers = 4 * owners
    subs = prec.shape[0]

    def rows_of(v):
        return v.reshape(dets, per_det, TILE).transpose(1, 0, 2).reshape(tiles, TILE)

    pix, ang = rows_of(pix), rows_of(ang)
    hit_row = hits.reshape(owners, 2).T.reshape(1, slots).astype(F32)
    me = jnp.stack([lax.axis_index("det"), lax.axis_index("tm"), owners]).astype(I32)

    binned = pl.pallas_call(
        bin_kernel,
        out_shape=jax.ShapeDtypeStruct((peers * 4, TILE), F32),
        in_specs=[SMEM, SMEM, VMEM, VMEM, VMEM],
        out_specs=VMEM,
        scratch_shapes=[
            pltpu.VMEM((tiles, TILE), F32),
            pltpu.VMEM((tiles, TILE), F32),
            pltpu.VMEM((slots // 2, 8, WINDOW), F32),
        ],
        name="bin_tiles",
    )(places, way, pix, ang, hit_row)
    binned = exchange(binned, 4)

    sky = pl.pallas_call(
        own_kernel,
        out_shape=jax.ShapeDtypeStruct((peers * 4, TILE), F32),
        in_specs=[SMEM, VMEM, VMEM],
        out_specs=VMEM,
        name="own_solve",
    )(me, binned, prec.transpose(1, 0, 2))
    sky = exchange(sky, 4)

    last = pl.pallas_call(
        scan_kernel,
        out_shape=jax.ShapeDtypeStruct((peers, TILE), F32),
        in_specs=[SMEM, SMEM, SMEM, VMEM, VMEM, VMEM],
        out_specs=VMEM,
        scratch_shapes=[
            pltpu.VMEM((tiles, TILE), F32),
            pltpu.VMEM((tiles, TILE), F32),
            pltpu.VMEM((slots // 2, 8, WINDOW), F32),
            pltpu.VMEM((8, TILE), F32),
        ],
        name="scan_tiles",
    )(places, way, res, pix, ang, sky)
    last = exchange(last, 1)

    return pl.pallas_call(
        end_kernel,
        out_shape=[jax.ShapeDtypeStruct(amp.shape, F32)] * 3,
        in_specs=[SMEM, VMEM, VMEM],
        out_specs=[VMEM] * 3,
        scratch_shapes=[pltpu.VMEM((2, peers, TILE), F32)],
        name="end_step",
    )(me, last, amp)


def solution(mesh):
    return jax.shard_map(
        shards,
        mesh=mesh,
        in_specs=(
            P("det", "tm"),
            P("det", "tm"),
            P("det", "tm"),
            P("det", "tm"),
            P("det", "tm"),
            P("det", "tm"),
            P("tm", "det", None, None),
            P("det", None, None),
        ),
        out_specs=(P("det", "tm"), P("det", "tm"), P("det", "tm")),
        check_vma=False,
    )
```

time: 787 us -> 98.3 us (0.12)
  waiting for transfers between devices: 287 us -> 19.8 us
  other arithmetic: 176 us -> 1.33 us
  local copies, waits for them, and re-layouts: 141 us -> 1.39 us
  blocking collectives: 148 us -> 46.3 us
  between operations: 16.7 us -> 0.65 us
  matrix products: 13.5 us -> 0 us
  Pallas kernels: 0 us -> 12.8 us
  starting transfers between devices: 3.64 us -> 15.6 us
    scatter-add x1 -> x0, other arithmetic: 170 us -> none  [shards(): jax.ops.segment_sum(values, targets, num_segments=slot_count * cells)]
    reduce_scatter x1 -> x0, waiting for transfers between devices: 155 us -> none  [shards(): owned = lax.psum_scatter(full_bins, 'det', scatter_dimension=0, tiled=True)]
    psum x2 -> x0, blocking collectives: 148 us -> none  [the longest x1 74.6 us: shards(): lax.psum((jnp.sum(system_remainder * system_remainder), jnp.sum(conjugate...]
    gather x6 -> x0, local copies, waits for them, and re-layouts: 137 us -> none  [the longest x2 45.6 us: shards(): flat_sky[cell + 2 * WINDOW]]
    all_gather x1 -> x0, waiting for transfers between devices: 80.8 us -> none  [shards(): whole_sky = lax.all_gather(sky_map, 'det', axis=0, tiled=True)]
    psum x1 -> x0, waiting for transfers between devices: 47.9 us -> none  [shards(): binned = lax.psum(owned, 'tm')]
    all_to_all x0 -> x2, blocking collectives: none -> 46.3 us  [exchange(): lax.all_to_all(value.reshape(peers, rows, TILE), AXES, 0, 0, tiled=True)]
    all_to_all x0 -> x1, waiting for transfers between devices: none -> 19.8 us  [exchange(): lax.all_to_all(value.reshape(peers, rows, TILE), AXES, 0, 0, tiled=True)]
  transfers between devices with their start and end apart: 5 -> 1, of which waited for: 4 -> 1; matrix products, arithmetic and copies ran while one was open for 0% -> 1% of each run, Pallas kernels for 0% -> 0%
where the time goes in v1:
time: 98.3 us; the launch traced here: 98 us
  blocking collectives  46.3 us (47%)
  waiting for transfers between devices  19.8 us (20%)
  starting transfers between devices  15.6 us (16%)
  Pallas kernels  12.8 us (13%)
  local copies, waits for them, and re-layouts  1.39 us (1%)
  other arithmetic  1.33 us (1%)
    all_to_all x2, blocking collectives, exchange(): lax.all_to_all(value.reshape(peers, rows, TILE), AXES, 0, 0, tiled=True)  46.3 us
    all_to_all x1, waiting for transfers between devices, exchange(): lax.all_to_all(value.reshape(peers, rows, TILE), AXES, 0, 0, tiled=True)  19.8 us
    all_to_all x1, starting transfers between devices, exchange(): lax.all_to_all(value.reshape(peers, rows, TILE), AXES, 0, 0, tiled=True)  15.6 us
    pallas_call x1, Pallas kernels, shards(): pl.pallas_call(scan_kernel, out_shape=jax.ShapeDtypeStruct((peers, TILE),...  4.14 us
    pallas_call x1, Pallas kernels, shards(): pl.pallas_call(bin_kernel, out_shape=jax.ShapeDtypeStruct((peers * 4, TIL...  4.01 us
    pallas_call x1, Pallas kernels, shards(): pl.pallas_call(own_kernel, out_shape=jax.ShapeDtypeStruct((peers * 4, TIL...  2.61 us
    pallas_call x1, Pallas kernels, shards(): pl.pallas_call(end_kernel, out_shape=[jax.ShapeDtypeStruct(amp.shape, F32...  2.05 us
  transfers between devices with their start and end apart: 1, of which 1 were waited for; matrix products, arithmetic and copies ran while one was open for 1% of the time, Pallas kernels for 0%

profile of v1, /device:TPU:1, one launch (start us, length us, event | category | flops | bytes accessed | tf_op | source)
XLA Modules:
  0.0 98.0 jit_solution(17746481123382317593)
XLA Ops:
  0.6 0.7 convert_bitcast_fusion
  1.3 0.6 convert_element_type.12.hits_ref
  1.9 4.0 %bin_tiles.1 = f32[1024,128]{1,0:T(8,128)} custom-call(s32[2,32]{1,0:T(2,128)} %slot_ref.3, f32[2,4]{1,0:T(2,128)} %dir_ref.3, s32[64,128]{1,0:T(8,128)} %bitcast.32, f32[64,128]{1,0:T(8,128)} %bitcast.34, f32[1,128]{1,0:T(1,128)} %convert_element_type.12.hits_ref), custom_call_target="tpu_custom_call" | custom-call | tf_op jit(solution)/shard_map/bin_tiles/pallas_call | solution.py:283
  5.9 15.6 %all-to-all-start = ((f32[256,4,128]{2,1,0:T(4,128)}), f32[256,4,128]{2,1,0:T(4,128)S(1)}, u32[]{:S(2)}, u32[]{:S(2)}) async-start(f32[256,4,128]{2,1,0:T(4,128)} %bitcast.27), calls=%async_computation | async-start | bytes 1048576 | tf_op jit(solution)/shard_map/all_to_all | solution.py:263
  21.6 0.7 pad_add_fusion.me_ref
  22.2 19.8 %all-to-all-done = f32[256,4,128]{2,1,0:T(4,128)S(1)} async-done(((f32[256,4,128]{2,1,0:T(4,128)}), f32[256,4,128]{2,1,0:T(4,128)S(1)}, u32[]{:S(2)}, u32[]{:S(2)}) %all-to-all-start) | async-done | bytes 524320 | tf_op jit(solution)/shard_map/all_to_all | solution.py:263
  42.1 0.0 copy-start
  42.1 0.8 copy-done
  42.9 2.6 %own_solve.1 = f32[1024,128]{1,0:T(8,128)} custom-call(s32[3]{0:T(128)} %pad_add_fusion.me_ref, f32[1024,128]{1,0:T(8,128)} %bitcast.25, f32[6,48,256]{2,1,0:T(8,128)} %bitcast.31), custom_call_target="tpu_custom_call" | custom-call | tf_op jit(solution)/shard_map/own_solve/pallas_call | solution.py:297
  45.5 26.8 %all_to_all.15 = f32[256,4,128]{2,1,0:T(4,128)} all-to-all(f32[256,4,128]{2,1,0:T(4,128)} %bitcast.26), channel_id=1, replica_groups=mesh['tm'=4,'det'=64] {'tm','det'}, dimensions={0} | all-to-all | bytes 1048576 | tf_op jit(solution)/shard_map/all_to_all | solution.py:263
  72.3 4.1 %scan_tiles.1 = f32[256,128]{1,0:T(8,128)} custom-call(s32[2,32]{1,0:T(2,128)} %slot_ref.3, f32[2,4]{1,0:T(2,128)} %dir_ref.3, f32[2,4]{1,0:T(2,128)} %res_ref.1, s32[64,128]{1,0:T(8,128)} %bitcast.33, f32[64,128]{1,0:T(8,128)} %bitcast.35, f32[1024,128]{1,0:T(8,128)} %bitcast.28), custom_call_target="tpu_custom_call" | custom-call | tf_op jit(solution)/shard_map/scan_tiles/pallas_call | solution.py:306
  76.4 19.5 %all_to_all.16 = f32[256,1,128]{2,1,0:T(1,128)} all-to-all(f32[256,1,128]{2,1,0:T(1,128)} %bitcast.30), channel_id=1, replica_groups=mesh['tm'=4,'det'=64] {'tm','det'}, dimensions={0} | all-to-all | bytes 262144 | tf_op jit(solution)/shard_map/all_to_all | solution.py:263
  95.9 2.0 %end_step.1 = (f32[2,4]{1,0:T(2,128)}, f32[2,4]{1,0:T(2,128)}, f32[2,4]{1,0:T(2,128)}) custom-call(s32[3]{0:T(128)} %pad_add_fusion.me_ref, f32[256,128]{1,0:T(8,128)} %bitcast.29, f32[2,4]{1,0:T(2,128)} %amp_ref.1), custom_call_target="tpu_custom_call" | custom-call | tf_op jit(solution)/shard_map/end_step/pallas_call | solution.py:321
Async XLA Ops:
  5.9 36.1 %all-to-all-start = ((f32[256,4,128]{2,1,0:T(4,128)}), f32[256,4,128]{2,1,0:T(4,128)S(1)}, u32[]{:S(2)}, u32[]{:S(2)}) async-start(f32[256,4,128]{2,1,0:T(4,128)} %bitcast.27), calls=%async_computation | async-start | bytes 1048576 | tf_op jit(solution)/shard_map/all_to_all | solution.py:263
  42.1 0.8 copy-start

commit v2 on v1

--- a/solution.py
+++ b/solution.py
@@ -1,5 +1,3 @@
-import functools
-
 import jax
 import jax.numpy as jnp
 import numpy as np
@@ -11,6 +9,16 @@
 TILE = 128
 WINDOW = 256
 STIFFNESS = 0.5
+
+ROOM = 23
+CHUNK = 2 * ROOM + 2
+CODES = 2 * ROOM
+HITS = 2 * ROOM + 1
+COUNT = 32
+OVER = 33
+WAYS = 40
+PLANES = 8
+NEAR = 8
 BF16 = jnp.bfloat16
 F32 = jnp.float32
 I32 = jnp.int32
@@ -50,50 +58,34 @@
     return cosine, sine
 
 
-def tile_parts(row, slot, pix_ref, cos_ref, sin_ref):
-    hot = iota((WINDOW, TILE), 0) == pix_ref[pl.ds(row, 1), :]
+def tile_parts(pixels, cosine, sine, half):
+    hot = iota((WINDOW, TILE), 0) == pixels
     hot = jnp.where(hot, 1.0, 0.0).astype(BF16)
     sub = iota((8, TILE), 0)
     part = sub & 3
-    weight = jnp.where(
-        part == 0, 1.0, jnp.where(part == 1, cos_ref[pl.ds(row, 1), :], sin_ref[pl.ds(row, 1), :])
-    )
-    mine = (sub >> 2) == ((slot >> 1) & 1)
-    weight = jnp.where(mine & (part < 3), weight, 0.0)
+    weight = jnp.where(part == 0, 1.0, jnp.where(part == 1, cosine, sine))
+    weight = jnp.where(((sub >> 2) == half) & (part < 3), weight, 0.0)
     return hot, weight
 
 
-def bin_kernel(slot_ref, dir_ref, pix_ref, ang_ref, hits_ref, out_ref, cos_ref, sin_ref, acc_ref):
-    c, s = cos_sin(2.0 * ang_ref[...])
-    cos_ref[...] = c
-    sin_ref[...] = s
-    acc_ref[...] = jnp.zeros_like(acc_ref)
-    tiles = pix_ref.shape[0]
-    dets, bases = dir_ref.shape
-    span = tiles // dets // bases
-
-    def group(g, carry):
-        det, base = g % dets, g // dets
-        height = dir_ref[det, base]
-        for t in range(span):
-            tile = base * span + t
-            slot = slot_ref[det, tile]
-            hot, weight = tile_parts(tile * dets + det, slot, pix_ref, cos_ref, sin_ref)
-            high = weight.astype(BF16).astype(F32)
-            both = jnp.concatenate([high, weight - high], axis=0).astype(BF16)
-            res = dot(both, hot, NT)
-            res = (res[:8] + res[8:]) * height
-            place = (slot & 1) * (acc_ref.shape[0] // 2) + (slot >> 2)
-            acc_ref[place] = acc_ref[place] + res
-        return carry
-
-    lax.fori_loop(0, dets * bases, group, 0)
-
+def bin_tile(hot, weight):
+    high = weight.astype(BF16).astype(F32)
+    both = jnp.concatenate([high, weight - high], axis=0).astype(BF16)
+    res = dot(both, hot, NT)
+    return res[:8] + res[8:]
+
+
+def scan_tile(hot, weight, value):
+    high = value.astype(BF16).astype(F32)
+    both = jnp.concatenate([high, value - high], axis=0).astype(BF16)
+    res = dot(both, hot)
+    return (res[:8] + res[8:]) * weight
+
+
+def put_bins(acc_ref, out_ref, extra):
     pairs = acc_ref.shape[0] // 2
-    sub = iota((8, TILE), 0)
     left = iota((8, TILE), 1) < 64
-    last = (sub & 3) == 3
-    hits = jnp.broadcast_to(hits_ref[...], (8, TILE))
+    last = (iota((8, TILE), 0) & 3) == 3
     for u in range(pairs):
         for b in range(2):
             first = acc_ref[u, :, b * TILE : (b + 1) * TILE]
@@ -102,7 +94,141 @@
             odd = jnp.where(left, pltpu.roll(first, 64, 1), second)
             for q, value in ((2 * b, even), (2 * b + 1, odd)):
                 at = (q * pairs + u) * 8
-                out_ref[at : at + 8, :] = jnp.where(last, hits, value)
+                out_ref[at : at + 8, :] = jnp.where(last, extra[u % len(extra)], value)
+
+
+def get_sky(in_ref, sky_ref):
+    pairs = sky_ref.shape[0] // 2
+    left = iota((8, TILE), 1) < 64
+    for u in range(pairs):
+        for b in range(2):
+            at = (2 * b * pairs + u) * 8
+            even = in_ref[at : at + 8, :]
+            at = ((2 * b + 1) * pairs + u) * 8
+            odd = in_ref[at : at + 8, :]
+            sky_ref[u, :, b * TILE : (b + 1) * TILE] = jnp.where(left, even, pltpu.roll(odd, 64, 1))
+            sky_ref[pairs + u, :, b * TILE : (b + 1) * TILE] = jnp.where(
+                left, pltpu.roll(even, 64, 1), odd
+            )
+
+
+def pack_kernel(slot_ref, way_ref, res_ref, amp_ref, pix_ref, ang_ref, hits_ref, out_ref, own_ref):
+    dets, bases = way_ref.shape
+    per_det = slot_ref.shape[1]
+    span = per_det // bases
+    lane1 = iota((1, TILE), 1)
+    values = jnp.zeros((1, TILE), F32)
+    amps = jnp.zeros((1, TILE), F32)
+    for d in range(dets):
+        for b in range(bases):
+            k = d * bases + b
+            values = jnp.where((lane1 == WAYS + k) | (lane1 == 72 + k), way_ref[d, b], values)
+            values = jnp.where(lane1 == 64 + k, res_ref[d, b], values)
+            amps = jnp.where(lane1 == k, amp_ref[d, b], amps)
+    own_ref[...] = jnp.zeros_like(own_ref)
+    own_ref[0:1, :] = values
+    own_ref[1:2, :] = amps
+
+    out_ref[...] = jnp.zeros_like(out_ref)
+    sub, lane = iota((PLANES, TILE), 0), iota((PLANES, TILE), 1)
+
+    def tile_step(t, carry):
+        low, high, codes = carry
+        for d in range(dets):
+            slot = slot_ref[d, t]
+            plane = slot // (2 * NEAR)
+            shift = (plane & 3) * 8
+            upper = plane >> 2
+            place = (jnp.where(upper == 1, high, low) >> shift) & 255
+            one = jnp.left_shift(jnp.int32(1), shift)
+            low = jnp.where(upper == 1, low, low + one)
+            high = jnp.where(upper == 1, high + one, high)
+            place = jnp.minimum(place, ROOM - 1)
+            row = t * dets + d
+            at = plane * CHUNK + place
+            out_ref[pl.ds(at, 1), :] = pix_ref[pl.ds(row, 1), :].astype(F32)
+            out_ref[pl.ds(at + ROOM, 1), :] = ang_ref[pl.ds(row, 1), :]
+            code = (slot & (2 * NEAR - 1)) * 8 + d * bases + t // span
+            codes = jnp.where((sub == plane) & (lane == place), code, codes)
+        return low, high, codes
+
+    zero = jnp.int32(0)
+    low, high, codes = lax.fori_loop(
+        0, per_det, tile_step, (zero, zero, jnp.zeros((PLANES, TILE), I32)), unroll=4
+    )
+    over = zero
+    for z in range(PLANES):
+        count = ((high if z >= 4 else low) >> (8 * (z & 3))) & 255
+        over = jnp.maximum(over, jnp.where(count > ROOM, 1, 0))
+        codes = jnp.where((sub == z) & (lane == COUNT), jnp.minimum(count, ROOM), codes)
+    codes = jnp.where(lane == OVER, over, codes)
+    codes = jnp.where(lane < WAYS, codes.astype(F32), values)
+    out_ref[pl.ds(CODES, PLANES, stride=CHUNK), :] = codes
+    hits = jnp.concatenate([hits_ref[0:1, :], hits_ref[1:2, :]], axis=1).astype(F32)
+    out_ref[pl.ds(HITS, PLANES, stride=CHUNK), :] = jnp.broadcast_to(hits, (PLANES, TILE))
+
+
+def start_codes(in_ref, code_ref, sems):
+    copies = [
+        pltpu.make_async_copy(
+            in_ref.at[pl.ds(z * CHUNK + CODES, 1), :], code_ref.at[pl.ds(z, 1), :], sems.at[z]
+        )
+        for z in range(PLANES)
+    ]
+    for copy in copies:
+        copy.start()
+    return copies
+
+
+def each_tile(in_ref, code_ref, cos_ref, sin_ref, use, group=4):
+    def source(z, carry):
+        count = code_ref[z, COUNT].astype(I32)
+
+        def some(g, carry):
+            for k in range(group):
+                p = g * group + k
+                code = code_ref[z, p].astype(I32)
+                base = code & 7
+                row = z * CHUNK + p
+                hot, weight = tile_parts(
+                    in_ref[pl.ds(row, 1), :].astype(I32),
+                    cos_ref[pl.ds(row + ROOM, 1), :],
+                    sin_ref[pl.ds(row + ROOM, 1), :],
+                    z & 1,
+                )
+                use(z, code >> 3, base, p < count, hot, weight)
+            return carry
+
+        return lax.fori_loop(0, (count + group - 1) // group, some, carry)
+
+    lax.fori_loop(0, PLANES, source, 0)
+
+
+def place_of(z, local):
+    return (local & 1) * (NEAR * PLANES // 2) + (local >> 1) * (PLANES // 2) + (z >> 1)
+
+
+def bin_kernel(in_ref, out_ref, cos_ref, sin_ref, acc_ref, code_ref, sems):
+    copies = start_codes(in_ref, code_ref, sems)
+    c, s = cos_sin(2.0 * in_ref[...])
+    cos_ref[...] = c
+    sin_ref[...] = s
+    acc_ref[...] = jnp.zeros_like(acc_ref)
+    for copy in copies:
+        copy.wait()
+
+    def use(z, local, base, valid, hot, weight):
+        height = jnp.where(valid, code_ref[z, WAYS + base], 0.0)
+        place = place_of(z, local)
+        acc_ref[place] = acc_ref[place] + bin_tile(hot, weight) * height
+
+    each_tile(in_ref, code_ref, cos_ref, sin_ref, use)
+    upper = iota((8, TILE), 0) < 4
+    hits = []
+    for z in range(0, PLANES, 2):
+        first, second = (in_ref[y * CHUNK + HITS : y * CHUNK + HITS + 1, :] for y in (z, z + 1))
+        hits.append(jnp.where(upper, first, second))
+    put_bins(acc_ref, out_ref, hits)
 
 
 def own_kernel(me_ref, in_ref, prec_ref, out_ref):
@@ -160,23 +286,130 @@
 
 
 def scan_kernel(
+    in_ref, sky_in_ref, own_ref, out_ref, cos_ref, sin_ref, sky_ref, sum_ref, code_ref, sems
+):
+    copies = start_codes(in_ref, code_ref, sems)
+    c, s = cos_sin(2.0 * in_ref[...])
+    cos_ref[...] = c
+    sin_ref[...] = s
+    get_sky(sky_in_ref, sky_ref)
+    sum_ref[...] = jnp.zeros_like(sum_ref)
+    for copy in copies:
+        copy.wait()
+
+    def use(z, local, base, valid, hot, weight):
+        res = scan_tile(hot, weight, sky_ref[place_of(z, local)])
+        sum_ref[z * 8 + base] = sum_ref[z * 8 + base] + res * jnp.where(valid, 1.0, 0.0)
+
+    each_tile(in_ref, code_ref, cos_ref, sin_ref, use)
+    count = PLANES * 8
+    sums = jnp.sum(jnp.sum(sum_ref[...], axis=1), axis=1, keepdims=True)
+    lane, sub = iota((count, TILE), 1), iota((count, TILE), 0)
+    row = jnp.sum(jnp.where(lane == sub, sums, 0.0), axis=0, keepdims=True)
+    row = row * np.float32(1.0 / 1024)
+    lane = iota((1, TILE), 1)
+    row = jnp.where(lane < 64, row, jnp.where(lane < 80, own_ref[0:1, :], 0.0))
+    over = code_ref[0, OVER]
+    for z in range(1, PLANES):
+        over = jnp.maximum(over, code_ref[z, OVER])
+    row = jnp.where(lane == 96, over, row)
+    out_ref[...] = jnp.broadcast_to(row, out_ref.shape)
+
+
+def end_kernel(me_ref, in_ref, own_ref, amp_out, res_out, dir_out, over_out, keep_ref):
+    dets, bases = amp_out.shape
+    spans = in_ref.shape[0] // (PLANES * NEAR)
+    lane = iota((NEAR, TILE), 1)
+    valid = lane < PLANES * 8
+    base = lane % bases
+    scan, way, rest = [], [], []
+    over = jnp.zeros((NEAR, TILE), F32)
+    for i in range(spans):
+        a = w = r = jnp.zeros((NEAR, TILE), F32)
+        for z in range(PLANES):
+            at = (i * PLANES + z) * NEAR
+            x = in_ref[at : at + NEAR, :]
+            a = a + x
+            over = jnp.maximum(over, x)
+            group = lane >> 3
+            r = r + pltpu.roll(jnp.where(group == 8, x, 0.0), (z * 8 - 64) % TILE, 1)
+            w = w + pltpu.roll(jnp.where(group == 9, x, 0.0), (z * 8 - 72) % TILE, 1)
+        scan.append(a)
+        way.append(w)
+        rest.append(r)
+    over = jnp.max(jnp.where(lane == 96, over, 0.0))
+    zero = jnp.zeros((NEAR, TILE), F32)
+    applied = []
+    for i in range(spans):
+        from_left = pltpu.roll(way[i - 1] if i else zero, TILE - (bases - 1), 1)
+        from_right = pltpu.roll(way[i + 1] if i < spans - 1 else zero, bases - 1, 1)
+        before = jnp.where(base == 0, from_left, pltpu.roll(way[i], 1, 1))
+        after = jnp.where(base == bases - 1, from_right, pltpu.roll(way[i], TILE - 1, 1))
+        v = scan[i] + way[i] + STIFFNESS * (2.0 * way[i] - before - after)
+        applied.append(jnp.where(valid, v, 0.0))
+
+    def total(terms):
+        v = terms[0]
+        for term in terms[1:]:
+            v = v + term
+        return jnp.sum(jnp.sum(v, axis=0, keepdims=True), axis=1, keepdims=True)
+
+    now = total([r * r for r in rest])
+    factor = now / total([w * a for w, a in zip(way, applied)])
+    fresh = [r - factor * a for r, a in zip(rest, applied)]
+    ratio = total([f * f for f in fresh]) / now
+    for i in range(spans):
+        keep_ref[i * NEAR : (i + 1) * NEAR, :] = fresh[i]
+    mine = jnp.broadcast_to(keep_ref[pl.ds(me_ref[1] * NEAR + me_ref[0] % NEAR, 1), :], (8, TILE))
+    mine = pltpu.roll(mine, (TILE - (me_ref[0] // NEAR) * 8) % TILE, 1)[0:1]
+    my_way = own_ref[0:1, 72:80]
+    my_fresh = mine[:, 0:8]
+    moved = own_ref[1:2, 0:8] + factor * my_way
+    turn = my_fresh + ratio * my_way
+    for d in range(dets):
+        lo, hi = d * bases, (d + 1) * bases
+        amp_out[d : d + 1, :] = moved[:, lo:hi]
+        res_out[d : d + 1, :] = my_fresh[:, lo:hi]
+        dir_out[d : d + 1, :] = turn[:, lo:hi]
+    over_out[0] = over
+
+
+def slow_bin_kernel(slot_ref, dir_ref, pix_ref, ang_ref, hits_ref, out_ref, cos_ref, sin_ref, acc_ref):
+    c, s = cos_sin(2.0 * ang_ref[...])
+    cos_ref[...] = c
+    sin_ref[...] = s
+    acc_ref[...] = jnp.zeros_like(acc_ref)
+    tiles = pix_ref.shape[0]
+    dets, bases = dir_ref.shape
+    span = tiles // dets // bases
+
+    def group(g, carry):
+        det, base = g % dets, g // dets
+        height = dir_ref[det, base]
+        for t in range(span):
+            tile = base * span + t
+            slot = slot_ref[det, tile]
+            row = pl.ds(tile * dets + det, 1)
+            hot, weight = tile_parts(
+                pix_ref[row, :], cos_ref[row, :], sin_ref[row, :], (slot >> 1) & 1
+            )
+            place = (slot & 1) * (acc_ref.shape[0] // 2) + (slot >> 2)
+            acc_ref[place] = acc_ref[place] + bin_tile(hot, weight) * height
+        return carry
+
+    lax.fori_loop(0, dets * bases, group, 0)
+
+    put_bins(acc_ref, out_ref, [jnp.broadcast_to(hits_ref[...], (8, TILE))])
+
+
+def slow_scan_kernel(
     slot_ref, dir_ref, res_ref, pix_ref, ang_ref, in_ref, out_ref, cos_ref, sin_ref, sky_ref, sum_ref
 ):
     c, s = cos_sin(2.0 * ang_ref[...])
     cos_ref[...] = c
     sin_ref[...] = s
+    get_sky(in_ref, sky_ref)
     pairs = sky_ref.shape[0] // 2
-    left = iota((8, TILE), 1) < 64
-    for u in range(pairs):
-        for b in range(2):
-            at = (2 * b * pairs + u) * 8
-            even = in_ref[at : at + 8, :]
-            at = ((2 * b + 1) * pairs + u) * 8
-            odd = in_ref[at : at + 8, :]
-            sky_ref[u, :, b * TILE : (b + 1) * TILE] = jnp.where(left, even, pltpu.roll(odd, 64, 1))
-            sky_ref[pairs + u, :, b * TILE : (b + 1) * TILE] = jnp.where(
-                left, pltpu.roll(even, 64, 1), odd
-            )
     tiles = pix_ref.shape[0]
     dets, bases = dir_ref.shape
     span = tiles // dets // bases
@@ -187,13 +420,12 @@
         for t in range(span):
             tile = base * span + t
             slot = slot_ref[det, tile]
-            hot, weight = tile_parts(tile * dets + det, slot, pix_ref, cos_ref, sin_ref)
+            row = pl.ds(tile * dets + det, 1)
+            hot, weight = tile_parts(
+                pix_ref[row, :], cos_ref[row, :], sin_ref[row, :], (slot >> 1) & 1
+            )
             place = (slot & 1) * pairs + (slot >> 2)
-            value = sky_ref[place]
-            high = value.astype(BF16).astype(F32)
-            both = jnp.concatenate([high, value - high], axis=0).astype(BF16)
-            res = dot(both, hot)
-            total = total + (res[:8] + res[8:]) * weight
+            total = total + scan_tile(hot, weight, sky_ref[place])
         sum_ref[pl.ds(det * bases + base, 1), :] = jnp.sum(total, axis=0, keepdims=True)
         return carry
 
@@ -211,7 +443,7 @@
     out_ref[...] = jnp.broadcast_to(row, out_ref.shape)
 
 
-def end_kernel(me_ref, in_ref, amp_ref, amp_out, res_out, dir_out, keep_ref):
+def slow_end_kernel(me_ref, in_ref, amp_ref, amp_out, res_out, dir_out, keep_ref):
     rows = in_ref.shape[0]
     dets, bases = amp_ref.shape
     count = dets * bases
@@ -255,13 +487,64 @@
 
 SMEM = pl.BlockSpec(memory_space=pltpu.SMEM)
 VMEM = pl.BlockSpec(memory_space=pltpu.VMEM)
-AXES = ("tm", "det")
-
-
-def exchange(value, rows):
+SMALL = pltpu.CompilerParams(vmem_limit_bytes=12 << 20)
+DET = ("z", "x", "core")
+ALL = ("tm",) + DET
+PLANE = ("tm", "x", "core")
+
+
+def exchange(value, axes, rows):
     peers = value.shape[0] // rows
-    moved = lax.all_to_all(value.reshape(peers, rows, TILE), AXES, 0, 0, tiled=True)
+    moved = lax.all_to_all(value.reshape(peers, rows, TILE), axes, 0, 0, tiled=True)
     return moved.reshape(value.shape)
+
+
+def f32(*shape):
+    return jax.ShapeDtypeStruct(shape, F32)
+
+
+def slow(me, amp, res, way, pix, ang, places, hits, prec):
+    tiles = pix.shape[0]
+    slots = hits.shape[1] * 2
+    peers = 4 * hits.shape[1]
+    hit_row = hits.reshape(1, slots).astype(F32)
+    table = [pltpu.VMEM((tiles, TILE), F32)] * 2 + [pltpu.VMEM((slots // 2, 8, WINDOW), F32)]
+    binned = pl.pallas_call(
+        slow_bin_kernel,
+        out_shape=f32(peers * 4, TILE),
+        in_specs=[SMEM, SMEM, VMEM, VMEM, VMEM],
+        out_specs=VMEM,
+        scratch_shapes=table,
+        name="slow_bin",
+    )(places, way, pix, ang, hit_row)
+    sky = solve(me, exchange(binned, ALL, 4), prec)
+    last = pl.pallas_call(
+        slow_scan_kernel,
+        out_shape=f32(peers, TILE),
+        in_specs=[SMEM, SMEM, SMEM, VMEM, VMEM, VMEM],
+        out_specs=VMEM,
+        scratch_shapes=table + [pltpu.VMEM((8, TILE), F32)],
+        name="slow_scan",
+    )(places, way, res, pix, ang, exchange(sky, ALL, 4))
+    return pl.pallas_call(
+        slow_end_kernel,
+        out_shape=[f32(*amp.shape)] * 3,
+        in_specs=[SMEM, VMEM, VMEM],
+        out_specs=[VMEM] * 3,
+        scratch_shapes=[pltpu.VMEM((2, peers, TILE), F32)],
+        name="slow_end",
+    )(me, exchange(last, ALL, 1), amp)
+
+
+def solve(me, binned, prec):
+    return pl.pallas_call(
+        own_kernel,
+        out_shape=f32(*binned.shape),
+        in_specs=[SMEM, VMEM, VMEM],
+        out_specs=VMEM,
+        compiler_params=SMALL,
+        name="own_solve",
+    )(me, binned, prec)
 
 
 def shards(amp, res, way, pix, ang, places, hits, prec):
@@ -269,79 +552,74 @@
     per_det = samples // TILE
     tiles = dets * per_det
     owners = hits.shape[2]
-    slots = owners * hits.shape[3]
     peers = 4 * owners
-    subs = prec.shape[0]
 
     def rows_of(v):
         return v.reshape(dets, per_det, TILE).transpose(1, 0, 2).reshape(tiles, TILE)
 
     pix, ang = rows_of(pix), rows_of(ang)
-    hit_row = hits.reshape(owners, 2).T.reshape(1, slots).astype(F32)
-    me = jnp.stack([lax.axis_index("det"), lax.axis_index("tm"), owners]).astype(I32)
-
+    hits = hits.reshape(owners, 2).T
+    prec = prec.transpose(1, 0, 2)
+    me = jnp.stack([lax.axis_index(DET), lax.axis_index("tm"), owners]).astype(I32)
+
+    packed, own = pl.pallas_call(
+        pack_kernel,
+        out_shape=[f32(PLANES * CHUNK, TILE), f32(8, TILE)],
+        in_specs=[SMEM, SMEM, SMEM, SMEM, VMEM, VMEM, VMEM],
+        out_specs=[VMEM, VMEM],
+        name="pack_tiles",
+    )(places, way, res, amp, pix, ang, hits)
+    packed = exchange(packed, "z", CHUNK)
+
+    angles = [pltpu.VMEM((PLANES * CHUNK, TILE), F32)] * 2
+    table = pltpu.VMEM((NEAR * PLANES, 8, WINDOW), F32)
+    codes = [pltpu.SMEM((PLANES, TILE), F32), pltpu.SemaphoreType.DMA((PLANES,))]
     binned = pl.pallas_call(
         bin_kernel,
-        out_shape=jax.ShapeDtypeStruct((peers * 4, TILE), F32),
-        in_specs=[SMEM, SMEM, VMEM, VMEM, VMEM],
+        out_shape=f32(peers * 4, TILE),
+        in_specs=[VMEM],
         out_specs=VMEM,
-        scratch_shapes=[
-            pltpu.VMEM((tiles, TILE), F32),
-            pltpu.VMEM((tiles, TILE), F32),
-            pltpu.VMEM((slots // 2, 8, WINDOW), F32),
-        ],
+        scratch_shapes=angles + [table] + codes,
+        compiler_params=SMALL,
         name="bin_tiles",
-    )(places, way, pix, ang, hit_row)
-    binned = exchange(binned, 4)
-
-    sky = pl.pallas_call(
-        own_kernel,
-        out_shape=jax.ShapeDtypeStruct((peers * 4, TILE), F32),
-        in_specs=[SMEM, VMEM, VMEM],
-        out_specs=VMEM,
-        name="own_solve",
-    )(me, binned, prec.transpose(1, 0, 2))
-    sky = exchange(sky, 4)
+    )(packed)
+    sky = solve(me, exchange(binned, PLANE, 4 * PLANES), prec)
+    sky = exchange(sky, PLANE, 4 * PLANES)
 
     last = pl.pallas_call(
         scan_kernel,
-        out_shape=jax.ShapeDtypeStruct((peers, TILE), F32),
-        in_specs=[SMEM, SMEM, SMEM, VMEM, VMEM, VMEM],
+        out_shape=f32(peers, TILE),
+        in_specs=[VMEM, VMEM, VMEM],
         out_specs=VMEM,
-        scratch_shapes=[
-            pltpu.VMEM((tiles, TILE), F32),
-            pltpu.VMEM((tiles, TILE), F32),
-            pltpu.VMEM((slots // 2, 8, WINDOW), F32),
-            pltpu.VMEM((8, TILE), F32),
-        ],
+        scratch_shapes=angles + [table, pltpu.VMEM((PLANES * 8, 8, TILE), F32)] + codes,
+        compiler_params=SMALL,
         name="scan_tiles",
-    )(places, way, res, pix, ang, sky)
-    last = exchange(last, 1)
-
-    return pl.pallas_call(
+    )(packed, sky, own)
+    *out, over = pl.pallas_call(
         end_kernel,
-        out_shape=[jax.ShapeDtypeStruct(amp.shape, F32)] * 3,
+        out_shape=[f32(*amp.shape)] * 3 + [f32(1)],
         in_specs=[SMEM, VMEM, VMEM],
-        out_specs=[VMEM] * 3,
-        scratch_shapes=[pltpu.VMEM((2, peers, TILE), F32)],
+        out_specs=[VMEM] * 3 + [SMEM],
+        scratch_shapes=[pltpu.VMEM((4 * NEAR, TILE), F32)],
+        compiler_params=SMALL,
         name="end_step",
-    )(me, last, amp)
+    )(me, exchange(last, ALL, 1), own)
+    return lax.cond(
+        over[0] > 0,
+        lambda: tuple(slow(me, amp, res, way, pix, ang, places, hits, prec)),
+        lambda: tuple(out),
+    )
 
 
 def solution(mesh):
+    spans = mesh.shape["tm"]
+    split_mesh = jax.sharding.Mesh(
+        mesh.devices.reshape(spans, PLANES, NEAR // 2, 2), ("tm", "z", "x", "core")
+    )
     return jax.shard_map(
         shards,
-        mesh=mesh,
-        in_specs=(
-            P("det", "tm"),
-            P("det", "tm"),
-            P("det", "tm"),
-            P("det", "tm"),
-            P("det", "tm"),
-            P("det", "tm"),
-            P("tm", "det", None, None),
-            P("det", None, None),
-        ),
-        out_specs=(P("det", "tm"), P("det", "tm"), P("det", "tm")),
+        mesh=split_mesh,
+        in_specs=(P(DET, "tm"),) * 6 + (P("tm", DET, None, None), P(DET, None, None)),
+        out_specs=(P(DET, "tm"),) * 3,
         check_vma=False,
     )

time: 98.3 us -> 91.8 us (0.934)
  blocking collectives: 46.3 us -> 33.1 us
  waiting for transfers between devices: 19.8 us -> 24.3 us
  Pallas kernels: 12.8 us -> 14.8 us
  other arithmetic: 1.33 us -> 0.08 us
  starting transfers between devices: 15.6 us -> 16.6 us
    all_to_all x2, blocking collectives: 46.3 us -> 33.1 us  [exchange(): lax.all_to_all(value.reshape(peers, rows, TILE), axes, 0, 0, tiled=True)]
    all_to_all x1 -> x2, waiting for transfers between devices: 19.8 us -> 24.3 us  [exchange(): lax.all_to_all(value.reshape(peers, rows, TILE), axes, 0, 0, tiled=True)]
    pallas_call x4 -> x5, Pallas kernels: 12.8 us -> 14.8 us  [the longest x1 5.15 us: shards(): pl.pallas_call(bin_kernel, out_shape=f32(peers * 4, TILE), in_specs=[VMEM...]
    all_to_all x1 -> x2, starting transfers between devices: 15.6 us -> 16.6 us  [exchange(): lax.all_to_all(value.reshape(peers, rows, TILE), axes, 0, 0, tiled=True)]
  transfers between devices with their start and end apart: 1 -> 2, of which waited for: 1 -> 2; matrix products, arithmetic and copies ran while one was open for 1% -> 0% of each run, Pallas kernels for 0% -> 0%
where the time goes in v2:
time: 91.8 us; the launch traced here: 90.9 us
  blocking collectives  33.1 us (36%)
  waiting for transfers between devices  24.3 us (26%)
  starting transfers between devices  16.6 us (18%)
  Pallas kernels  14.8 us (16%)
  between operations  1.4 us (2%)
    all_to_all x2, blocking collectives, exchange(): lax.all_to_all(value.reshape(peers, rows, TILE), axes, 0, 0, tiled=True)  33.1 us
    all_to_all x2, waiting for transfers between devices, exchange(): lax.all_to_all(value.reshape(peers, rows, TILE), axes, 0, 0, tiled=True)  24.3 us
    all_to_all x2, starting transfers between devices, exchange(): lax.all_to_all(value.reshape(peers, rows, TILE), axes, 0, 0, tiled=True)  16.6 us
    pallas_call x1, Pallas kernels, shards(): pl.pallas_call(bin_kernel, out_shape=f32(peers * 4, TILE), in_specs=[VMEM...  5.15 us
    pallas_call x1, Pallas kernels, shards(): pl.pallas_call(scan_kernel, out_shape=f32(peers, TILE), in_specs=[VMEM, V...  4.33 us
    pallas_call x1, Pallas kernels, shards(): pl.pallas_call(pack_kernel, out_shape=[f32(PLANES * CHUNK, TILE), f32(8,...  2.45 us
  transfers between devices with their start and end apart: 2, of which 2 were waited for; matrix products, arithmetic and copies ran while one was open for 0% of the time, Pallas kernels for 0%

profile of v2, /device:TPU:1, one launch (start us, length us, event | category | flops | bytes accessed | tf_op | source)
XLA Modules:
  0.0 90.9 jit_solution(9954478084125814461)
XLA Ops:
  0.6 0.0 copy-start.7
  0.6 0.0 copy-start.8
  0.7 0.0 copy-start.5
  0.7 0.0 copy-start.6
  0.7 0.0 copy-start.4
  0.7 0.6 copy-done.7
  1.3 0.0 copy-done.8
  1.3 0.0 copy-done.5
  1.3 0.0 copy-done.6
  1.4 0.0 copy-done.4
  1.4 2.5 %pack_tiles.1 = (f32[384,128]{1,0:T(8,128)}, f32[8,128]{1,0:T(8,128)}) custom-call(s32[2,32]{1,0:T(2,128)S(1)} %copy-done.4, f32[2,4]{1,0:T(2,128)S(1)} %copy-done.5, f32[2,4]{1,0:T(2,128)S(1)} %copy-done.6, f32[2,4]{1,0:T(2,128)S(1)} %copy-done.7, s32[64,128]{1,0:T(8,128)} %bitcast.49, f32[64,128]{1,0:T(8,128)} %bitcast.51, s32[2,64]{1,0:T(2,128)S(1)} %bitcast.54), custom_call_target="tpu_custom_call" | custom-call | tf_op jit(solution)/shard_map/pack_tiles/pallas_call | solution.py:565
  3.8 18.0 %all_to_all.35 = f32[8,48,128]{2,1,0:T(8,128)S(1)} all-to-all(f32[8,48,128]{2,1,0:T(8,128)} %bitcast.53), channel_id=1, replica_groups=mesh['tm'=4,'z'=8,'x'=4,'core'=2] {'z'}, dimensions={0} | all-to-all | bytes 393216 | tf_op jit(solution)/shard_map/all_to_all | solution.py:498
  21.8 5.1 %bin_tiles.1 = f32[1024,128]{1,0:T(8,128)} custom-call(f32[384,128]{1,0:T(8,128)S(1)} %bitcast.40), custom_call_target="tpu_custom_call" | custom-call | tf_op jit(solution)/shard_map/bin_tiles/pallas_call | solution.py:577
  27.0 0.0 copy-start.1
  27.0 10.8 %all-to-all-start.4 = ((f32[32,32,128]{2,1,0:T(8,128)}), f32[32,32,128]{2,1,0:T(8,128)S(1)}, u32[]{:S(2)}, u32[]{:S(2)}) async-start(f32[32,32,128]{2,1,0:T(8,128)} %bitcast.20), calls=%async_computation.4 | async-start | bytes 1048576 | tf_op jit(solution)/shard_map/all_to_all | solution.py:498
  37.8 0.1 pad_add_fusion.me_ref
  37.8 11.3 %all-to-all-done.4 = f32[32,32,128]{2,1,0:T(8,128)S(1)} async-done(((f32[32,32,128]{2,1,0:T(8,128)}), f32[32,32,128]{2,1,0:T(8,128)S(1)}, u32[]{:S(2)}, u32[]{:S(2)}) %all-to-all-start.4) | async-done | bytes 524320 | tf_op jit(solution)/shard_map/all_to_all | solution.py:498
  49.2 0.0 copy-done.1
  49.2 1.2 %own_solve.3 = f32[1024,128]{1,0:T(8,128)S(1)} custom-call(s32[3]{0:T(128)S(1)} %pad_add_fusion.me_ref, f32[1024,128]{1,0:T(8,128)S(1)} %bitcast.35, f32[6,48,256]{2,1,0:T(8,128)S(1)} %bitcast.45), custom_call_target="tpu_custom_call" | custom-call | tf_op jit(solution)/shard_map/own_solve/pallas_call | solution.py:540
  50.4 0.0 copy-start
  50.4 15.1 %all_to_all.36 = f32[32,32,128]{2,1,0:T(8,128)S(1)} all-to-all(f32[32,32,128]{2,1,0:T(8,128)S(1)} %bitcast.36), channel_id=1, replica_groups=mesh['tm'=4,'z'=8,'x'=4,'core'=2] {'tm','x','core'}, dimensions={0} | all-to-all | bytes 1048576 | tf_op jit(solution)/shard_map/all_to_all | solution.py:498
  65.5 0.0 copy-done
  65.5 4.3 %scan_tiles.1 = f32[256,128]{1,0:T(8,128)} custom-call(f32[384,128]{1,0:T(8,128)S(1)} %bitcast.41, f32[1024,128]{1,0:T(8,128)S(1)} %bitcast.39, f32[8,128]{1,0:T(8,128)S(1)} %copy-done), custom_call_target="tpu_custom_call" | custom-call | tf_op jit(solution)/shard_map/scan_tiles/pallas_call | solution.py:589
  69.8 5.9 %all-to-all-start.6 = ((f32[256,1,128]{2,1,0:T(1,128)}), f32[256,1,128]{2,1,0:T(1,128)S(1)}, u32[]{:S(2)}, u32[]{:S(2)}) async-start(f32[256,1,128]{2,1,0:T(1,128)} %bitcast.26), calls=%async_computation.6 | async-start | bytes 262144 | tf_op jit(solution)/shard_map/all_to_all | solution.py:498
  75.7 12.9 %all-to-all-done.6 = f32[256,1,128]{2,1,0:T(1,128)S(1)} async-done(((f32[256,1,128]{2,1,0:T(1,128)}), f32[256,1,128]{2,1,0:T(1,128)S(1)}, u32[]{:S(2)}, u32[]{:S(2)}) %all-to-all-start.6) | async-done | bytes 131104 | tf_op jit(solution)/shard_map/all_to_all | solution.py:498
  88.7 0.0 copy-start.2
  88.7 0.0 copy-start.3
  88.7 1.6 %end_step.1 = (f32[2,4]{1,0:T(2,128)}, f32[2,4]{1,0:T(2,128)}, f32[2,4]{1,0:T(2,128)}, f32[1]{0:T(128)}) custom-call(s32[3]{0:T(128)S(1)} %pad_add_fusion.me_ref, f32[256,128]{1,0:T(8,128)S(1)} %bitcast.42, f32[8,128]{1,0:T(8,128)S(1)} %copy-done), custom_call_target="tpu_custom_call" | custom-call | tf_op jit(solution)/shard_map/end_step/pallas_call | solution.py:598
  90.9 0.0 copy-done.2
  90.9 0.0 copy-done.3
  (1 shorter events, 0.0 us)
Async XLA Ops:
  0.6 0.7 copy-start.7
  0.6 0.7 copy-start.8
  0.7 0.7 copy-start.5
  0.7 0.7 copy-start.6
  0.7 0.7 copy-start.4
  27.0 22.2 %copy-start.1 = (f32[48,6,256]{2,0,1:T(8,128)S(1)}, f32[48,6,256]{2,0,1:T(8,128)}, u32[]{:S(2)}) copy-start(f32[48,6,256]{2,0,1:T(8,128)} %param.17) | copy-start | bytes 884740
  27.0 22.2 %all-to-all-start.4 = ((f32[32,32,128]{2,1,0:T(8,128)}), f32[32,32,128]{2,1,0:T(8,128)S(1)}, u32[]{:S(2)}, u32[]{:S(2)}) async-start(f32[32,32,128]{2,1,0:T(8,128)} %bitcast.20), calls=%async_computation.4 | async-start | bytes 1048576 | tf_op jit(solution)/shard_map/all_to_all | solution.py:498
  50.4 15.1 %copy-start = (f32[8,128]{1,0:T(8,128)S(1)}, f32[8,128]{1,0:T(8,128)}, u32[]{:S(2)}) copy-start(f32[8,128]{1,0:T(8,128)} %get-tuple-element.43.own_ref) | copy-start | bytes 12292
  69.8 18.8 %all-to-all-start.6 = ((f32[256,1,128]{2,1,0:T(1,128)}), f32[256,1,128]{2,1,0:T(1,128)S(1)}, u32[]{:S(2)}, u32[]{:S(2)}) async-start(f32[256,1,128]{2,1,0:T(1,128)} %bitcast.26), calls=%async_computation.6 | async-start | bytes 262144 | tf_op jit(solution)/shard_map/all_to_all | solution.py:498
  88.7 2.3 %copy-start.2 = (s32[2,4096]{1,0:T(2,128)S(1)}, s32[2,4096]{1,0:T(2,128)}, u32[]{:S(2)}) copy-start(s32[2,4096]{1,0:T(2,128)} %param.13) | copy-start | bytes 98308
  88.7 2.3 %copy-start.3 = (f32[2,4096]{1,0:T(2,128)S(1)}, f32[2,4096]{1,0:T(2,128)}, u32[]{:S(2)}) copy-start(f32[2,4096]{1,0:T(2,128)} %param.14) | copy-start | bytes 98308

commit v3 on v2

--- a/solution.py
+++ b/solution.py
@@ -14,6 +14,7 @@
 CHUNK = 2 * ROOM + 2
 CODES = 2 * ROOM
 HITS = 2 * ROOM + 1
+ANGLES = 24
 COUNT = 32
 OVER = 33
 WAYS = 40
@@ -112,7 +113,17 @@
             )
 
 
-def pack_kernel(slot_ref, way_ref, res_ref, amp_ref, pix_ref, ang_ref, hits_ref, out_ref, own_ref):
+def pack_kernel(*refs):
+    slot_ref, way_ref, res_ref, amp_ref, pix_ref, ang_ref, hits_ref = refs[9:16]
+    out_ref, own_ref = refs[7:9]
+    sems = refs[16]
+    copies = [pltpu.make_async_copy(refs[k], refs[9 + k], sems.at[k]) for k in range(7)]
+    for copy in copies:
+        copy.start()
+    own_ref[...] = jnp.zeros_like(own_ref)
+    out_ref[...] = jnp.zeros_like(out_ref)
+    for copy in copies:
+        copy.wait()
     dets, bases = way_ref.shape
     per_det = slot_ref.shape[1]
     span = per_det // bases
@@ -125,11 +136,8 @@
             values = jnp.where((lane1 == WAYS + k) | (lane1 == 72 + k), way_ref[d, b], values)
             values = jnp.where(lane1 == 64 + k, res_ref[d, b], values)
             amps = jnp.where(lane1 == k, amp_ref[d, b], amps)
-    own_ref[...] = jnp.zeros_like(own_ref)
     own_ref[0:1, :] = values
     own_ref[1:2, :] = amps
-
-    out_ref[...] = jnp.zeros_like(out_ref)
     sub, lane = iota((PLANES, TILE), 0), iota((PLANES, TILE), 1)
 
     def tile_step(t, carry):
@@ -146,9 +154,11 @@
             place = jnp.minimum(place, ROOM - 1)
             row = t * dets + d
             at = plane * CHUNK + place
-            out_ref[pl.ds(at, 1), :] = pix_ref[pl.ds(row, 1), :].astype(F32)
-            out_ref[pl.ds(at + ROOM, 1), :] = ang_ref[pl.ds(row, 1), :]
-            code = (slot & (2 * NEAR - 1)) * 8 + d * bases + t // span
+            out_ref[pl.ds(at, 1), :] = ang_ref[pl.ds(row, 1), :]
+            pixels = pix_ref[pl.ds(row, 1), :] ^ ((slot & 1) * 64)
+            out_ref[pl.ds(at + ROOM, 1), :] = pixels.astype(F32)
+            block = (slot & 1) * NEAR + ((slot >> 1) & (NEAR - 1))
+            code = block * 8 + d * bases + t // span
             codes = jnp.where((sub == plane) & (lane == place), code, codes)
         return low, high, codes
 
@@ -169,77 +179,125 @@
 
 
 def start_codes(in_ref, code_ref, sems):
+    name_in, way_in = in_ref
+    names, ways = code_ref
     copies = [
-        pltpu.make_async_copy(
-            in_ref.at[pl.ds(z * CHUNK + CODES, 1), :], code_ref.at[pl.ds(z, 1), :], sems.at[z]
+        pltpu.make_async_copy(name_in, names, sems.at[PLANES]),
+    ]
+    for z in range(PLANES):
+        copies.append(
+            pltpu.make_async_copy(
+                way_in.at[pl.ds(z * CHUNK + CODES, 1), :], ways.at[pl.ds(z, 1), :], sems.at[z]
+            )
         )
-        for z in range(PLANES)
-    ]
     for copy in copies:
         copy.start()
     return copies
 
 
-def each_tile(in_ref, code_ref, cos_ref, sin_ref, use, group=4):
-    def source(z, carry):
-        count = code_ref[z, COUNT].astype(I32)
-
-        def some(g, carry):
-            for k in range(group):
-                p = g * group + k
-                code = code_ref[z, p].astype(I32)
-                base = code & 7
-                row = z * CHUNK + p
-                hot, weight = tile_parts(
-                    in_ref[pl.ds(row, 1), :].astype(I32),
-                    cos_ref[pl.ds(row + ROOM, 1), :],
-                    sin_ref[pl.ds(row + ROOM, 1), :],
-                    z & 1,
-                )
-                use(z, code >> 3, base, p < count, hot, weight)
-            return carry
-
-        return lax.fori_loop(0, (count + group - 1) // group, some, carry)
-
-    lax.fori_loop(0, PLANES, source, 0)
-
-
-def place_of(z, local):
-    return (local & 1) * (NEAR * PLANES // 2) + (local >> 1) * (PLANES // 2) + (z >> 1)
-
-
-def bin_kernel(in_ref, out_ref, cos_ref, sin_ref, acc_ref, code_ref, sems):
-    copies = start_codes(in_ref, code_ref, sems)
-    c, s = cos_sin(2.0 * in_ref[...])
-    cos_ref[...] = c
-    sin_ref[...] = s
+def each_tile(in_ref, names, cos_ref, sin_ref, use):
+    part = iota((8, TILE), 0) & 3
+    first, second, real = part == 0, part == 1, part < 3
+    pixel = iota((WINDOW, TILE), 0).astype(F32).astype(BF16)
+    counts = [names[z, COUNT] for z in range(PLANES)]
+    steps = jnp.int32(0)
+    for z in range(0, PLANES, 2):
+        steps = jnp.maximum(steps, (counts[z] + counts[z + 1] + 1) // 2)
+
+    def some(g, carry):
+        for k in range(PLANES):
+            even = k // 2 * 2
+            i = g * 2 + k % 2
+            valid = i < counts[even] + counts[even + 1]
+            other = i >= counts[even]
+            z = even + jnp.where(other, 1, 0)
+            p = jnp.minimum(jnp.where(other, i - counts[even], i), ROOM - 1)
+            code = names[z, p]
+            mine = in_ref[pl.ds(z * CHUNK + ROOM + p, 1), :]
+            mine = jnp.broadcast_to(mine, (WINDOW, TILE)).astype(BF16)
+            hot = jnp.maximum(1.0 - jnp.abs(pixel - mine), 0.0)
+            row = pl.ds(z * ANGLES + p, 1)
+            weight = jnp.where(first, 1.0, jnp.where(second, cos_ref[row, :], sin_ref[row, :]))
+            use(z, code >> 3, code & 7, valid, hot, jnp.where(real, weight, 0.0))
+        return carry
+
+    lax.fori_loop(0, steps, some, 0)
+
+
+def table_rows(z, block):
+    return pl.ds(block * (4 * PLANES) + z, 4, stride=PLANES)
+
+
+def bin_kernel(in_ref, name_ref, out_ref, cos_ref, sin_ref, acc_ref, names, ways, sems):
+    copies = start_codes((name_ref, in_ref), (names, ways), sems)
+    for z in range(PLANES):
+        c, s = cos_sin(2.0 * in_ref[z * CHUNK : z * CHUNK + ANGLES, :])
+        cos_ref[z * ANGLES : (z + 1) * ANGLES, :] = c
+        sin_ref[z * ANGLES : (z + 1) * ANGLES, :] = s
     acc_ref[...] = jnp.zeros_like(acc_ref)
     for copy in copies:
         copy.wait()
-
-    def use(z, local, base, valid, hot, weight):
-        height = jnp.where(valid, code_ref[z, WAYS + base], 0.0)
-        place = place_of(z, local)
-        acc_ref[place] = acc_ref[place] + bin_tile(hot, weight) * height
-
-    each_tile(in_ref, code_ref, cos_ref, sin_ref, use)
     upper = iota((8, TILE), 0) < 4
-    hits = []
-    for z in range(0, PLANES, 2):
-        first, second = (in_ref[y * CHUNK + HITS : y * CHUNK + HITS + 1, :] for y in (z, z + 1))
-        hits.append(jnp.where(upper, first, second))
-    put_bins(acc_ref, out_ref, hits)
+
+    def use(z, block, base, valid, hot, weight):
+        height = jnp.where(valid, ways[z, WAYS + base], 0.0)
+        high = weight.astype(BF16).astype(F32)
+        both = jnp.where(upper, high, weight - high).astype(BF16)
+        res = dot(both, hot, NT)
+        rows = table_rows(z, block)
+        for b in range(2):
+            cols = slice(b * TILE, (b + 1) * TILE)
+            acc_ref[b, rows, :] = acc_ref[b, rows, :] + (res[:4, cols] + res[4:, cols]) * height
+
+    each_tile(in_ref, names, cos_ref, sin_ref, use)
+    left = iota((8, TILE), 1) < 64
+    hits = in_ref[pl.ds(HITS, PLANES, stride=CHUNK), :]
+    for xc in range(NEAR):
+        for c in range(4):
+            for b in range(2):
+                first = acc_ref[b, (xc * 4 + c) * 8 : (xc * 4 + c + 1) * 8, :]
+                second = acc_ref[b, ((NEAR + xc) * 4 + c) * 8 : ((NEAR + xc) * 4 + c + 1) * 8, :]
+                for h, value in (
+                    (0, jnp.where(left, first, second)),
+                    (1, jnp.where(left, second, first)),
+                ):
+                    at = (((2 * b + h) * NEAR + xc) * 4 + c) * 8
+                    out_ref[at : at + 8, :] = hits if c == 3 else value
 
 
 def own_kernel(me_ref, in_ref, prec_ref, out_ref):
-    me = me_ref[0]
-    quarter = me_ref[1]
+    peers = in_ref.shape[0]
+    sources = peers * PLANES
+
+    def take(c):
+        return in_ref[:, c * PLANES : (c + 1) * PLANES, :].reshape(sources, TILE)
+
+    def put(c, value):
+        out_ref[:, c * PLANES : (c + 1) * PLANES, :] = value.reshape(peers, PLANES, TILE)
+
+    own_solve(me_ref[0], me_ref[1], sources, take, prec_ref, put, 1)
+
+
+def slow_own_kernel(me_ref, in_ref, prec_ref, out_ref):
     sources = in_ref.shape[0] // 4
+
+    def take(c):
+        return in_ref[pl.ds(c, sources, stride=4), :]
+
+    def put(c, value):
+        out_ref[pl.ds(c, sources, stride=4), :] = value
+
+    own_solve(me_ref[0], me_ref[1], sources, take, prec_ref, put, 0)
+    put(3, jnp.zeros((sources, TILE), F32))
+
+
+def own_solve(me, quarter, sources, take, prec_ref, put, swap):
+    odd = (quarter % 2) * swap
     subs = prec_ref.shape[1]
-    ids = in_ref[pl.ds(3, sources, stride=4), :].astype(BF16)
+    ids = take(3).astype(BF16)
     lane = iota((16, TILE), 1)
     row = iota((16, TILE), 0)
-    pick = jnp.where((lane == me + 64 * row) & (row < 2), 1.0, 0.0).astype(BF16)
+    pick = jnp.where((lane == me + 64 * (row ^ odd)) & (row < 2), 1.0, 0.0).astype(BF16)
     id_rows = dot(pick, ids, NT).astype(I32)
     sub = iota((subs, sources), 0)
     hot = jnp.concatenate(
@@ -252,7 +310,7 @@
     left = iota((subs, TILE), 1) < 64
     binned = []
     for c in range(3):
-        high, low = split(in_ref[pl.ds(c, sources, stride=4), :])
+        high, low = split(take(c))
         res = dot(hot, jnp.concatenate([high, low], axis=1))
         res = res[:, :TILE] + res[:, TILE:]
         res = jnp.where(left, res[:subs], res[subs:])
@@ -272,7 +330,7 @@
     ]
 
     deep, wide = iota((TILE, TILE), 0), iota((TILE, TILE), 1)
-    spread = jnp.where(deep == me + (wide & 64), 1.0, 0.0).astype(BF16)
+    spread = jnp.where(deep == me + ((wide & 64) ^ (64 * odd)), 1.0, 0.0).astype(BF16)
     named = dot(ids, spread).astype(I32)
     back = jnp.where(named == (iota((sources, TILE), 1) & 63), 1.0, 0.0).astype(BF16)
     back = jnp.concatenate([back, back], axis=1)
@@ -281,27 +339,43 @@
         first = jnp.where(left, sky[c], 0.0)
         second = jnp.where(left, 0.0, sky[c])
         high, low = split(jnp.concatenate([first, gap, second, gap], axis=0))
-        out_ref[pl.ds(c, sources, stride=4), :] = dot(back, jnp.concatenate([high, low], axis=0))
-    out_ref[pl.ds(3, sources, stride=4), :] = jnp.zeros((sources, TILE), F32)
+        put(c, dot(back, jnp.concatenate([high, low], axis=0)))
 
 
 def scan_kernel(
-    in_ref, sky_in_ref, own_ref, out_ref, cos_ref, sin_ref, sky_ref, sum_ref, code_ref, sems
+    in_ref, name_ref, cos_ref, sin_ref, sky_in_ref, own_ref, out_ref, sky_ref, sum_ref, names, sems
 ):
-    copies = start_codes(in_ref, code_ref, sems)
-    c, s = cos_sin(2.0 * in_ref[...])
-    cos_ref[...] = c
-    sin_ref[...] = s
-    get_sky(sky_in_ref, sky_ref)
+    copy = pltpu.make_async_copy(name_ref, names, sems.at[0])
+    copy.start()
+    left = iota((8, TILE), 1) < 64
+    for xc in range(NEAR):
+        for c in range(3):
+            for b in range(2):
+                at = ((2 * b * NEAR + xc) * 3 + c) * 8
+                even = sky_in_ref[at : at + 8, :]
+                at = (((2 * b + 1) * NEAR + xc) * 3 + c) * 8
+                odd = sky_in_ref[at : at + 8, :]
+                at = (xc * 4 + c) * 8
+                sky_ref[b, at : at + 8, :] = jnp.where(left, even, odd)
+                at = ((NEAR + xc) * 4 + c) * 8
+                sky_ref[b, at : at + 8, :] = jnp.where(left, odd, even)
+    for block in range(2 * NEAR):
+        at = (block * 4 + 3) * 8
+        for b in range(2):
+            sky_ref[b, at : at + 8, :] = jnp.zeros((8, TILE), F32)
     sum_ref[...] = jnp.zeros_like(sum_ref)
-    for copy in copies:
-        copy.wait()
-
-    def use(z, local, base, valid, hot, weight):
-        res = scan_tile(hot, weight, sky_ref[place_of(z, local)])
-        sum_ref[z * 8 + base] = sum_ref[z * 8 + base] + res * jnp.where(valid, 1.0, 0.0)
-
-    each_tile(in_ref, code_ref, cos_ref, sin_ref, use)
+    copy.wait()
+
+    def use(z, block, base, valid, hot, weight):
+        rows = table_rows(z, block)
+        value = jnp.concatenate([sky_ref[0, rows, :], sky_ref[1, rows, :]], axis=1)
+        high = value.astype(BF16).astype(F32)
+        both = jnp.concatenate([high, value - high], axis=0).astype(BF16)
+        res = dot(both, hot) * weight
+        at = z * 8 + base
+        sum_ref[at] = sum_ref[at] + res * jnp.where(valid, 1.0, 0.0)
+
+    each_tile(in_ref, names, cos_ref, sin_ref, use)
     count = PLANES * 8
     sums = jnp.sum(jnp.sum(sum_ref[...], axis=1), axis=1, keepdims=True)
     lane, sub = iota((count, TILE), 1), iota((count, TILE), 0)
@@ -309,10 +383,10 @@
     row = row * np.float32(1.0 / 1024)
     lane = iota((1, TILE), 1)
     row = jnp.where(lane < 64, row, jnp.where(lane < 80, own_ref[0:1, :], 0.0))
-    over = code_ref[0, OVER]
+    over = names[0, OVER]
     for z in range(1, PLANES):
-        over = jnp.maximum(over, code_ref[z, OVER])
-    row = jnp.where(lane == 96, over, row)
+        over = jnp.maximum(over, names[z, OVER])
+    row = jnp.where(lane == 96, over.astype(F32), row)
     out_ref[...] = jnp.broadcast_to(row, out_ref.shape)
 
 
@@ -517,7 +591,7 @@
         scratch_shapes=table,
         name="slow_bin",
     )(places, way, pix, ang, hit_row)
-    sky = solve(me, exchange(binned, ALL, 4), prec)
+    sky = solve(slow_own_kernel, (me, exchange(binned, ALL, 4), prec), peers * 4)
     last = pl.pallas_call(
         slow_scan_kernel,
         out_shape=f32(peers, TILE),
@@ -536,15 +610,16 @@
     )(me, exchange(last, ALL, 1), amp)
 
 
-def solve(me, binned, prec):
+def solve(kernel, args, *shape):
+    shape = shape + (TILE,)
     return pl.pallas_call(
-        own_kernel,
-        out_shape=f32(*binned.shape),
+        kernel,
+        out_shape=f32(*shape),
         in_specs=[SMEM, VMEM, VMEM],
         out_specs=VMEM,
         compiler_params=SMALL,
-        name="own_solve",
-    )(me, binned, prec)
+        name=kernel.__name__,
+    )(*args)
 
 
 def shards(amp, res, way, pix, ang, places, hits, prec):
@@ -553,6 +628,7 @@
     tiles = dets * per_det
     owners = hits.shape[2]
     peers = 4 * owners
+    near = 4 * NEAR
 
     def rows_of(v):
         return v.reshape(dets, per_det, TILE).transpose(1, 0, 2).reshape(tiles, TILE)
@@ -565,36 +641,58 @@
     packed, own = pl.pallas_call(
         pack_kernel,
         out_shape=[f32(PLANES * CHUNK, TILE), f32(8, TILE)],
-        in_specs=[SMEM, SMEM, SMEM, SMEM, VMEM, VMEM, VMEM],
+        in_specs=[pl.BlockSpec(memory_space=pltpu.HBM)] * 7,
         out_specs=[VMEM, VMEM],
+        scratch_shapes=[
+            pltpu.SMEM(places.shape, I32),
+            pltpu.SMEM(way.shape, F32),
+            pltpu.SMEM(way.shape, F32),
+            pltpu.SMEM(way.shape, F32),
+            pltpu.VMEM((tiles, TILE), I32),
+            pltpu.VMEM((tiles, TILE), F32),
+            pltpu.VMEM(hits.shape, I32),
+            pltpu.SemaphoreType.DMA((7,)),
+        ],
+        compiler_params=SMALL,
         name="pack_tiles",
     )(places, way, res, amp, pix, ang, hits)
     packed = exchange(packed, "z", CHUNK)
 
-    angles = [pltpu.VMEM((PLANES * CHUNK, TILE), F32)] * 2
-    table = pltpu.VMEM((NEAR * PLANES, 8, WINDOW), F32)
-    codes = [pltpu.SMEM((PLANES, TILE), F32), pltpu.SemaphoreType.DMA((PLANES,))]
-    binned = pl.pallas_call(
+    table = pltpu.VMEM((2, 2 * NEAR * 4 * PLANES, TILE), F32)
+    names = packed.reshape(PLANES, CHUNK, TILE)[:, CODES].astype(I32)
+    sems = pltpu.SemaphoreType.DMA((PLANES + 1,))
+    binned, cosine, sine = pl.pallas_call(
         bin_kernel,
-        out_shape=f32(peers * 4, TILE),
-        in_specs=[VMEM],
-        out_specs=VMEM,
-        scratch_shapes=angles + [table] + codes,
+        out_shape=[f32(near * 4 * PLANES, TILE)] + [f32(PLANES * ANGLES, TILE)] * 2,
+        in_specs=[VMEM] * 2,
+        out_specs=[VMEM] * 3,
+        scratch_shapes=[
+            table,
+            pltpu.SMEM((PLANES, TILE), I32),
+            pltpu.SMEM((PLANES, TILE), F32),
+            sems,
+        ],
         compiler_params=SMALL,
         name="bin_tiles",
-    )(packed)
-    sky = solve(me, exchange(binned, PLANE, 4 * PLANES), prec)
-    sky = exchange(sky, PLANE, 4 * PLANES)
+    )(packed, names)
+    binned = exchange(binned, PLANE, 4 * PLANES).reshape(near, 4 * PLANES, TILE)
+    sky = solve(own_kernel, (me, binned, prec), near, 3 * PLANES)
+    sky = exchange(sky.reshape(near * 3 * PLANES, TILE), PLANE, 3 * PLANES)
 
     last = pl.pallas_call(
         scan_kernel,
         out_shape=f32(peers, TILE),
-        in_specs=[VMEM, VMEM, VMEM],
+        in_specs=[VMEM] * 6,
         out_specs=VMEM,
-        scratch_shapes=angles + [table, pltpu.VMEM((PLANES * 8, 8, TILE), F32)] + codes,
+        scratch_shapes=[
+            table,
+            pltpu.VMEM((PLANES * 8, 8, TILE), F32),
+            pltpu.SMEM((PLANES, TILE), I32),
+            sems,
+        ],
         compiler_params=SMALL,
         name="scan_tiles",
-    )(packed, sky, own)
+    )(packed, names, cosine, sine, sky, own)
     *out, over = pl.pallas_call(
         end_kernel,
         out_shape=[f32(*amp.shape)] * 3 + [f32(1)],

time: 91.8 us -> 86.5 us (0.942)
  starting transfers between devices: 16.6 us -> 14.7 us
  Pallas kernels: 14.8 us -> 13.1 us
  blocking collectives: 33.1 us -> 31.6 us
    all_to_all x2, starting transfers between devices: 16.6 us -> 14.7 us  [exchange(): lax.all_to_all(value.reshape(peers, rows, TILE), axes, 0, 0, tiled=True)]
    all_to_all x2, blocking collectives: 33.1 us -> 31.6 us  [exchange(): lax.all_to_all(value.reshape(peers, rows, TILE), axes, 0, 0, tiled=True)]
    pallas_call x3, Pallas kernels: 10.7 us -> 9.55 us  [the longest x1 4.52 us: shards(): pl.pallas_call(bin_kernel, out_shape=[f32(near * 4 * PLANES, TILE)] + [f3...]
where the time goes in v3:
time: 86.5 us; the launch traced here: 85.9 us
  blocking collectives  31.6 us (37%)
  waiting for transfers between devices  24.3 us (28%)
  starting transfers between devices  14.7 us (17%)
  Pallas kernels  13.1 us (15%)
  between operations  1.4 us (2%)
    all_to_all x2, blocking collectives, exchange(): lax.all_to_all(value.reshape(peers, rows, TILE), axes, 0, 0, tiled=True)  31.6 us
    all_to_all x2, waiting for transfers between devices, exchange(): lax.all_to_all(value.reshape(peers, rows, TILE), axes, 0, 0, tiled=True)  24.3 us
    all_to_all x2, starting transfers between devices, exchange(): lax.all_to_all(value.reshape(peers, rows, TILE), axes, 0, 0, tiled=True)  14.7 us
    pallas_call x1, Pallas kernels, shards(): pl.pallas_call(bin_kernel, out_shape=[f32(near * 4 * PLANES, TILE)] + [f3...  4.52 us
    pallas_call x1, Pallas kernels, shards(): pl.pallas_call(scan_kernel, out_shape=f32(peers, TILE), in_specs=[VMEM] *...  3.82 us
    pallas_call x1, Pallas kernels, shards(): pl.pallas_call(pack_kernel, out_shape=[f32(PLANES * CHUNK, TILE), f32(8,...  1.97 us
  transfers between devices with their start and end apart: 2, of which 2 were waited for; matrix products, arithmetic and copies ran while one was open for 0% of the time, Pallas kernels for 0%

profile of v3, /device:TPU:1, one launch (start us, length us, event | category | flops | bytes accessed | tf_op | source)
XLA Modules:
  0.0 85.9 jit_solution(763084747101367871)
XLA Ops:
  0.6 0.0 copy-start.6
  0.6 0.0 copy-start.7
  0.7 0.0 copy-start.4
  0.7 0.0 copy-start.5
  0.7 0.0 copy-start.3
  0.7 0.6 copy-done.6
  1.3 0.0 copy-done.7
  1.3 0.0 copy-done.4
  1.3 0.0 copy-done.5
  1.4 0.0 copy-done.3
  1.4 2.0 %pack_tiles.1 = (f32[384,128]{1,0:T(8,128)S(1)}, f32[8,128]{1,0:T(8,128)S(1)}) custom-call(s32[2,32]{1,0:T(2,128)S(1)} %copy-done.3, f32[2,4]{1,0:T(2,128)S(1)} %copy-done.4, f32[2,4]{1,0:T(2,128)S(1)} %copy-done.5, f32[2,4]{1,0:T(2,128)S(1)} %copy-done.6, s32[64,128]{1,0:T(8,128)} %bitcast.49, f32[64,128]{1,0:T(8,128)} %bitcast.51, s32[2,64]{1,0:T(2,128)S(1)} %bitcast.54), custom_call_target="tpu_custom_call" | custom-call | tf_op jit(solution)/shard_map/pack_tiles/pallas_call | solution.py:641
  3.3 17.8 %all_to_all.35 = f32[8,48,128]{2,1,0:T(8,128)S(1)} all-to-all(f32[8,48,128]{2,1,0:T(8,128)S(1)} %bitcast.42), channel_id=1, replica_groups=mesh['tm'=4,'z'=8,'x'=4,'core'=2] {'z'}, dimensions={0} | all-to-all | bytes 393216 | tf_op jit(solution)/shard_map/all_to_all | solution.py:572
  21.2 4.5 %bin_tiles.1 = (f32[1024,128]{1,0:T(8,128)}, f32[192,128]{1,0:T(8,128)S(1)}, f32[192,128]{1,0:T(8,128)S(1)}) custom-call(f32[384,128]{1,0:T(8,128)S(1)} %bitcast.38, s32[8,128]{1,0:T(8,128)S(1)} %convert_bitcast_fusion.name_ref), custom_call_target="tpu_custom_call" | custom-call | tf_op jit(solution)/shard_map/bin_tiles/pallas_call | solution.py:664
  25.7 0.0 copy-start
  25.7 9.4 %all-to-all-start.4 = ((f32[32,32,128]{2,1,0:T(8,128)}), f32[32,32,128]{2,1,0:T(8,128)S(1)}, u32[]{:S(2)}, u32[]{:S(2)}) async-start(f32[32,32,128]{2,1,0:T(8,128)} %bitcast.21), calls=%async_computation.4 | async-start | bytes 1048576 | tf_op jit(solution)/shard_map/all_to_all | solution.py:572
  35.1 0.1 pad_add_fusion.me_ref
  35.2 11.3 %all-to-all-done.4.in_ref = f32[32,32,128]{2,1,0:T(8,128)S(1)} async-done(((f32[32,32,128]{2,1,0:T(8,128)}), f32[32,32,128]{2,1,0:T(8,128)S(1)}, u32[]{:S(2)}, u32[]{:S(2)}) %all-to-all-start.4) | async-done | bytes 524320 | tf_op jit(solution)/shard_map/all_to_all | solution.py:572
  46.5 0.0 copy-done
  46.5 1.2 %own_kernel.1 = f32[32,24,128]{2,1,0:T(8,128)S(1)} custom-call(s32[3]{0:T(128)S(1)} %pad_add_fusion.me_ref, f32[32,32,128]{2,1,0:T(8,128)S(1)} %all-to-all-done.4.in_ref, f32[6,48,256]{2,1,0:T(8,128)S(1)} %bitcast.45), custom_call_target="tpu_custom_call" | custom-call | tf_op jit(solution)/shard_map/own_kernel/pallas_call | solution.py:615
  47.8 13.8 %all_to_all.36 = f32[32,24,128]{2,1,0:T(8,128)S(1)} all-to-all(f32[32,24,128]{2,1,0:T(8,128)S(1)} %own_kernel.1), channel_id=1, replica_groups=mesh['tm'=4,'z'=8,'x'=4,'core'=2] {'tm','x','core'}, dimensions={0} | all-to-all | bytes 786432 | tf_op jit(solution)/shard_map/all_to_all | solution.py:572
  61.5 3.8 %scan_tiles.1 = f32[256,128]{1,0:T(8,128)} custom-call(f32[384,128]{1,0:T(8,128)S(1)} %bitcast.39, s32[8,128]{1,0:T(8,128)S(1)} %convert_bitcast_fusion.name_ref, f32[192,128]{1,0:T(8,128)S(1)} %get-tuple-element.46.cos_ref, f32[192,128]{1,0:T(8,128)S(1)} %get-tuple-element.47.sin_ref, f32[768,128]{1,0:T(8,128)S(1)} %bitcast.40, ...), custom_call_target="tpu_custom_call" | custom-call | tf_op jit(solution)/shard_map/scan_tiles/pallas_call | solution.py:682
  65.4 5.3 %all-to-all-start.6 = ((f32[256,1,128]{2,1,0:T(1,128)}), f32[256,1,128]{2,1,0:T(1,128)S(1)}, u32[]{:S(2)}, u32[]{:S(2)}) async-start(f32[256,1,128]{2,1,0:T(1,128)} %bitcast.25), calls=%async_computation.6 | async-start | bytes 262144 | tf_op jit(solution)/shard_map/all_to_all | solution.py:572
  70.6 12.9 %all-to-all-done.6 = f32[256,1,128]{2,1,0:T(1,128)S(1)} async-done(((f32[256,1,128]{2,1,0:T(1,128)}), f32[256,1,128]{2,1,0:T(1,128)S(1)}, u32[]{:S(2)}, u32[]{:S(2)}) %all-to-all-start.6) | async-done | bytes 131104 | tf_op jit(solution)/shard_map/all_to_all | solution.py:572
  83.6 0.0 copy-start.1
  83.6 0.0 copy-start.2
  83.6 1.6 %end_step.1 = (f32[2,4]{1,0:T(2,128)}, f32[2,4]{1,0:T(2,128)}, f32[2,4]{1,0:T(2,128)}, f32[1]{0:T(128)}) custom-call(s32[3]{0:T(128)S(1)} %pad_add_fusion.me_ref, f32[256,128]{1,0:T(8,128)S(1)} %bitcast.41, f32[8,128]{1,0:T(8,128)S(1)} %get-tuple-element.49.own_ref), custom_call_target="tpu_custom_call" | custom-call | tf_op jit(solution)/shard_map/end_step/pallas_call | solution.py:696
  85.8 0.0 copy-done.1
  85.9 0.0 copy-done.2
  (3 shorter events, 0.0 us)
Async XLA Ops:
  0.6 0.7 copy-start.6
  0.6 0.7 copy-start.7
  0.7 0.7 copy-start.4
  0.7 0.7 copy-start.5
  0.7 0.7 copy-start.3
  25.7 20.9 %copy-start = (f32[48,6,256]{2,0,1:T(8,128)S(1)}, f32[48,6,256]{2,0,1:T(8,128)}, u32[]{:S(2)}) copy-start(f32[48,6,256]{2,0,1:T(8,128)} %param.17) | copy-start | bytes 884740
  25.7 20.8 %all-to-all-start.4 = ((f32[32,32,128]{2,1,0:T(8,128)}), f32[32,32,128]{2,1,0:T(8,128)S(1)}, u32[]{:S(2)}, u32[]{:S(2)}) async-start(f32[32,32,128]{2,1,0:T(8,128)} %bitcast.21), calls=%async_computation.4 | async-start | bytes 1048576 | tf_op jit(solution)/shard_map/all_to_all | solution.py:572
  65.4 18.2 %all-to-all-start.6 = ((f32[256,1,128]{2,1,0:T(1,128)}), f32[256,1,128]{2,1,0:T(1,128)S(1)}, u32[]{:S(2)}, u32[]{:S(2)}) async-start(f32[256,1,128]{2,1,0:T(1,128)} %bitcast.25), calls=%async_computation.6 | async-start | bytes 262144 | tf_op jit(solution)/shard_map/all_to_all | solution.py:572
  83.6 2.3 %copy-start.1 = (s32[2,4096]{1,0:T(2,128)S(1)}, s32[2,4096]{1,0:T(2,128)}, u32[]{:S(2)}) copy-start(s32[2,4096]{1,0:T(2,128)} %param.13) | copy-start | bytes 98308
  83.6 2.3 %copy-start.2 = (f32[2,4096]{1,0:T(2,128)S(1)}, f32[2,4096]{1,0:T(2,128)}, u32[]{:S(2)}) copy-start(f32[2,4096]{1,0:T(2,128)} %param.14) | copy-start | bytes 98308

commit v4 on v3

--- a/solution.py
+++ b/solution.py
@@ -15,6 +15,8 @@
 CODES = 2 * ROOM
 HITS = 2 * ROOM + 1
 ANGLES = 24
+GROUP = 4
+PER_STEP = 8
 COUNT = 32
 OVER = 33
 WAYS = 40
@@ -113,6 +115,11 @@
             )
 
 
+def coded(number):
+    base = number & 7
+    return (number >> 3) * 128 + (base >> 2) + (base & 3) * 16
+
+
 def pack_kernel(*refs):
     slot_ref, way_ref, res_ref, amp_ref, pix_ref, ang_ref, hits_ref = refs[9:16]
     out_ref, own_ref = refs[7:9]
@@ -126,7 +133,6 @@
         copy.wait()
     dets, bases = way_ref.shape
     per_det = slot_ref.shape[1]
-    span = per_det // bases
     lane1 = iota((1, TILE), 1)
     values = jnp.zeros((1, TILE), F32)
     amps = jnp.zeros((1, TILE), F32)
@@ -139,6 +145,8 @@
     own_ref[0:1, :] = values
     own_ref[1:2, :] = amps
     sub, lane = iota((PLANES, TILE), 0), iota((PLANES, TILE), 1)
+    pix = pix_ref[...]
+    pix_ref[...] = ((pix & 192) << 1) + (pix & 63)
 
     def tile_step(t, carry):
         low, high, codes = carry
@@ -155,11 +163,9 @@
             row = t * dets + d
             at = plane * CHUNK + place
             out_ref[pl.ds(at, 1), :] = ang_ref[pl.ds(row, 1), :]
-            pixels = pix_ref[pl.ds(row, 1), :] ^ ((slot & 1) * 64)
+            pixels = pix_ref[pl.ds(row, 1), :] + (slot & 1) * 64
             out_ref[pl.ds(at + ROOM, 1), :] = pixels.astype(F32)
-            block = (slot & 1) * NEAR + ((slot >> 1) & (NEAR - 1))
-            code = block * 8 + d * bases + t // span
-            codes = jnp.where((sub == plane) & (lane == place), code, codes)
+            codes = jnp.where((sub == plane) & (lane == place), slot * 64 + row, codes)
         return low, high, codes
 
     zero = jnp.int32(0)
@@ -170,8 +176,8 @@
     for z in range(PLANES):
         count = ((high if z >= 4 else low) >> (8 * (z & 3))) & 255
         over = jnp.maximum(over, jnp.where(count > ROOM, 1, 0))
-        codes = jnp.where((sub == z) & (lane == COUNT), jnp.minimum(count, ROOM), codes)
-    codes = jnp.where(lane == OVER, over, codes)
+        codes = jnp.where((sub == z) & (lane == COUNT), coded(jnp.minimum(count, ROOM)), codes)
+    codes = jnp.where(lane == OVER, coded(over), codes)
     codes = jnp.where(lane < WAYS, codes.astype(F32), values)
     out_ref[pl.ds(CODES, PLANES, stride=CHUNK), :] = codes
     hits = jnp.concatenate([hits_ref[0:1, :], hits_ref[1:2, :]], axis=1).astype(F32)
@@ -195,74 +201,78 @@
     return copies
 
 
-def each_tile(in_ref, names, cos_ref, sin_ref, use):
-    part = iota((8, TILE), 0) & 3
-    first, second, real = part == 0, part == 1, part < 3
-    pixel = iota((WINDOW, TILE), 0).astype(F32).astype(BF16)
+def each_pair(in_ref, names, cos_ref, sin_ref, use):
+    part, quarter = iota((16, TILE), 0) & 3, iota((16, TILE), 0) >> 2
+    first, second = part == 0, part == 1
+    quarter = jnp.where(part < 3, quarter, -1)
+    pixel = iota((TILE, TILE), 0).astype(F32).astype(BF16)
     counts = [names[z, COUNT] for z in range(PLANES)]
+    ends = []
+    for z in range(PLANES):
+        ends.append(counts[z] if z % GROUP == 0 else ends[-1] + counts[z])
     steps = jnp.int32(0)
-    for z in range(0, PLANES, 2):
-        steps = jnp.maximum(steps, (counts[z] + counts[z + 1] + 1) // 2)
+    for z in range(GROUP - 1, PLANES, GROUP):
+        steps = jnp.maximum(steps, (ends[z] + PER_STEP - 1) // PER_STEP)
+
+    def tile(group, i):
+        low = group * GROUP
+        z, start = jnp.int32(low), jnp.int32(0)
+        for k in range(GROUP - 1):
+            z = z + jnp.where(i >= ends[low + k], 1, 0)
+            start = jnp.where(i >= ends[low + k], ends[low + k], start)
+        p = jnp.minimum(i - start, ROOM - 1)
+        code = names[z, p]
+        mine = in_ref[pl.ds(z * CHUNK + ROOM + p, 1), :].astype(I32)
+        place = jnp.broadcast_to((mine & 127).astype(F32), (TILE, TILE)).astype(BF16)
+        hot = jnp.maximum(1.0 - jnp.abs(pixel - place), 0.0)
+        row = pl.ds(z * ANGLES + p, 1)
+        weight = jnp.where(first, 1.0, jnp.where(second, cos_ref[row, :], sin_ref[row, :]))
+        weight = jnp.where(quarter == (mine >> 7), weight, 0.0)
+        return (z, code >> 3, code & 7, i < ends[low + GROUP - 1]), hot, weight
 
     def some(g, carry):
-        for k in range(PLANES):
-            even = k // 2 * 2
-            i = g * 2 + k % 2
-            valid = i < counts[even] + counts[even + 1]
-            other = i >= counts[even]
-            z = even + jnp.where(other, 1, 0)
-            p = jnp.minimum(jnp.where(other, i - counts[even], i), ROOM - 1)
-            code = names[z, p]
-            mine = in_ref[pl.ds(z * CHUNK + ROOM + p, 1), :]
-            mine = jnp.broadcast_to(mine, (WINDOW, TILE)).astype(BF16)
-            hot = jnp.maximum(1.0 - jnp.abs(pixel - mine), 0.0)
-            row = pl.ds(z * ANGLES + p, 1)
-            weight = jnp.where(first, 1.0, jnp.where(second, cos_ref[row, :], sin_ref[row, :]))
-            use(z, code >> 3, code & 7, valid, hot, jnp.where(real, weight, 0.0))
+        for group in range(PLANES // GROUP):
+            for k in range(0, PER_STEP, 2):
+                use(*zip(*(tile(group, g * PER_STEP + k + n) for n in range(2))))
         return carry
 
     lax.fori_loop(0, steps, some, 0)
 
 
-def table_rows(z, block):
-    return pl.ds(block * (4 * PLANES) + z, 4, stride=PLANES)
-
-
-def bin_kernel(in_ref, name_ref, out_ref, cos_ref, sin_ref, acc_ref, names, ways, sems):
+def table_rows(q, owner, z):
+    return pl.ds((q * NEAR + owner) * (4 * PLANES) + z, 4, stride=PLANES)
+
+
+def halves(x):
+    high, low = split(x)
+    return jnp.concatenate([high, low], axis=0)
+
+
+def bin_kernel(in_ref, name_ref, out_ref, cos_ref, sin_ref, names, ways, sems):
     copies = start_codes((name_ref, in_ref), (names, ways), sems)
     for z in range(PLANES):
         c, s = cos_sin(2.0 * in_ref[z * CHUNK : z * CHUNK + ANGLES, :])
         cos_ref[z * ANGLES : (z + 1) * ANGLES, :] = c
         sin_ref[z * ANGLES : (z + 1) * ANGLES, :] = s
-    acc_ref[...] = jnp.zeros_like(acc_ref)
+    hits = in_ref[pl.ds(HITS, PLANES, stride=CHUNK), :]
+    for at in range(0, out_ref.shape[0], PLANES):
+        last = at // PLANES % 4 == 3
+        out_ref[at : at + PLANES, :] = hits if last else jnp.zeros((PLANES, TILE), F32)
     for copy in copies:
         copy.wait()
-    upper = iota((8, TILE), 0) < 4
-
-    def use(z, block, base, valid, hot, weight):
-        height = jnp.where(valid, ways[z, WAYS + base], 0.0)
-        high = weight.astype(BF16).astype(F32)
-        both = jnp.where(upper, high, weight - high).astype(BF16)
-        res = dot(both, hot, NT)
-        rows = table_rows(z, block)
-        for b in range(2):
-            cols = slice(b * TILE, (b + 1) * TILE)
-            acc_ref[b, rows, :] = acc_ref[b, rows, :] + (res[:4, cols] + res[4:, cols]) * height
-
-    each_tile(in_ref, names, cos_ref, sin_ref, use)
-    left = iota((8, TILE), 1) < 64
-    hits = in_ref[pl.ds(HITS, PLANES, stride=CHUNK), :]
-    for xc in range(NEAR):
-        for c in range(4):
-            for b in range(2):
-                first = acc_ref[b, (xc * 4 + c) * 8 : (xc * 4 + c + 1) * 8, :]
-                second = acc_ref[b, ((NEAR + xc) * 4 + c) * 8 : ((NEAR + xc) * 4 + c + 1) * 8, :]
-                for h, value in (
-                    (0, jnp.where(left, first, second)),
-                    (1, jnp.where(left, second, first)),
-                ):
-                    at = (((2 * b + h) * NEAR + xc) * 4 + c) * 8
-                    out_ref[at : at + 8, :] = hits if c == 3 else value
+
+    def use(tiles, hots, weights):
+        both = jnp.concatenate([halves(weight) for weight in weights], axis=0)
+        res = dot(both, jnp.concatenate(hots, axis=0), NT)
+        for n, (z, owner, base, valid) in enumerate(tiles):
+            height = jnp.where(valid, ways[z, WAYS + base], 0.0)
+            mine = res[32 * n : 32 * n + 32, n * TILE : (n + 1) * TILE]
+            mine = (mine[:16] + mine[16:]) * height
+            for q in range(4):
+                rows = table_rows(q, owner, z)
+                out_ref[rows, :] = out_ref[rows, :] + mine[4 * q : 4 * q + 4]
+
+    each_pair(in_ref, names, cos_ref, sin_ref, use)
 
 
 def own_kernel(me_ref, in_ref, prec_ref, out_ref):
@@ -275,7 +285,7 @@
     def put(c, value):
         out_ref[:, c * PLANES : (c + 1) * PLANES, :] = value.reshape(peers, PLANES, TILE)
 
-    own_solve(me_ref[0], me_ref[1], sources, take, prec_ref, put, 1)
+    own_solve(me_ref[0], me_ref[1], sources, take, prec_ref, put)
 
 
 def slow_own_kernel(me_ref, in_ref, prec_ref, out_ref):
@@ -287,17 +297,16 @@
     def put(c, value):
         out_ref[pl.ds(c, sources, stride=4), :] = value
 
-    own_solve(me_ref[0], me_ref[1], sources, take, prec_ref, put, 0)
+    own_solve(me_ref[0], me_ref[1], sources, take, prec_ref, put)
     put(3, jnp.zeros((sources, TILE), F32))
 
 
-def own_solve(me, quarter, sources, take, prec_ref, put, swap):
-    odd = (quarter % 2) * swap
+def own_solve(me, quarter, sources, take, prec_ref, put):
     subs = prec_ref.shape[1]
     ids = take(3).astype(BF16)
     lane = iota((16, TILE), 1)
     row = iota((16, TILE), 0)
-    pick = jnp.where((lane == me + 64 * (row ^ odd)) & (row < 2), 1.0, 0.0).astype(BF16)
+    pick = jnp.where((lane == me + 64 * row) & (row < 2), 1.0, 0.0).astype(BF16)
     id_rows = dot(pick, ids, NT).astype(I32)
     sub = iota((subs, sources), 0)
     hot = jnp.concatenate(
@@ -330,7 +339,7 @@
     ]
 
     deep, wide = iota((TILE, TILE), 0), iota((TILE, TILE), 1)
-    spread = jnp.where(deep == me + ((wide & 64) ^ (64 * odd)), 1.0, 0.0).astype(BF16)
+    spread = jnp.where(deep == me + (wide & 64), 1.0, 0.0).astype(BF16)
     named = dot(ids, spread).astype(I32)
     back = jnp.where(named == (iota((sources, TILE), 1) & 63), 1.0, 0.0).astype(BF16)
     back = jnp.concatenate([back, back], axis=1)
@@ -347,35 +356,29 @@
 ):
     copy = pltpu.make_async_copy(name_ref, names, sems.at[0])
     copy.start()
-    left = iota((8, TILE), 1) < 64
-    for xc in range(NEAR):
-        for c in range(3):
-            for b in range(2):
-                at = ((2 * b * NEAR + xc) * 3 + c) * 8
-                even = sky_in_ref[at : at + 8, :]
-                at = (((2 * b + 1) * NEAR + xc) * 3 + c) * 8
-                odd = sky_in_ref[at : at + 8, :]
-                at = (xc * 4 + c) * 8
-                sky_ref[b, at : at + 8, :] = jnp.where(left, even, odd)
-                at = ((NEAR + xc) * 4 + c) * 8
-                sky_ref[b, at : at + 8, :] = jnp.where(left, odd, even)
-    for block in range(2 * NEAR):
-        at = (block * 4 + 3) * 8
-        for b in range(2):
-            sky_ref[b, at : at + 8, :] = jnp.zeros((8, TILE), F32)
+    for peer in range(4 * NEAR):
+        for c in range(4):
+            at = (peer * 4 + c) * PLANES
+            here = (peer * 3 + c) * PLANES
+            sky_ref[at : at + PLANES, :] = (
+                sky_in_ref[here : here + PLANES, :] if c < 3 else jnp.zeros((PLANES, TILE), F32)
+            )
     sum_ref[...] = jnp.zeros_like(sum_ref)
     copy.wait()
 
-    def use(z, block, base, valid, hot, weight):
-        rows = table_rows(z, block)
-        value = jnp.concatenate([sky_ref[0, rows, :], sky_ref[1, rows, :]], axis=1)
-        high = value.astype(BF16).astype(F32)
-        both = jnp.concatenate([high, value - high], axis=0).astype(BF16)
-        res = dot(both, hot) * weight
-        at = z * 8 + base
-        sum_ref[at] = sum_ref[at] + res * jnp.where(valid, 1.0, 0.0)
-
-    each_tile(in_ref, names, cos_ref, sin_ref, use)
+    def use(tiles, hots, weights):
+        both = []
+        for z, owner, _, _ in tiles:
+            value = [sky_ref[table_rows(q, owner, z), :] for q in range(4)]
+            both.append(halves(jnp.concatenate(value, axis=0)))
+        res = dot(jnp.concatenate(both, axis=0), jnp.concatenate(hots, axis=1))
+        for n, (z, _, base, valid) in enumerate(tiles):
+            mine = res[32 * n : 32 * n + 32, n * TILE : (n + 1) * TILE]
+            mine = (mine[:16] + mine[16:]) * weights[n]
+            at = z * 8 + base
+            sum_ref[at] = sum_ref[at] + (mine[:8] + mine[8:]) * jnp.where(valid, 1.0, 0.0)
+
+    each_pair(in_ref, names, cos_ref, sin_ref, use)
     count = PLANES * 8
     sums = jnp.sum(jnp.sum(sum_ref[...], axis=1), axis=1, keepdims=True)
     lane, sub = iota((count, TILE), 1), iota((count, TILE), 0)
@@ -638,6 +641,7 @@
     prec = prec.transpose(1, 0, 2)
     me = jnp.stack([lax.axis_index(DET), lax.axis_index("tm"), owners]).astype(I32)
 
+    me, places = lax.optimization_barrier((me, places))
     packed, own = pl.pallas_call(
         pack_kernel,
         out_shape=[f32(PLANES * CHUNK, TILE), f32(8, TILE)],
@@ -658,8 +662,10 @@
     )(places, way, res, amp, pix, ang, hits)
     packed = exchange(packed, "z", CHUNK)
 
-    table = pltpu.VMEM((2, 2 * NEAR * 4 * PLANES, TILE), F32)
-    names = packed.reshape(PLANES, CHUNK, TILE)[:, CODES].astype(I32)
+    raw = packed.reshape(PLANES, CHUNK, TILE)[:, CODES].astype(I32)
+    slot, row = raw >> 6, raw & 63
+    base = row % dets * way.shape[1] + row // (tiles // way.shape[1])
+    names = (slot // 2 % NEAR) * 8 + base
     sems = pltpu.SemaphoreType.DMA((PLANES + 1,))
     binned, cosine, sine = pl.pallas_call(
         bin_kernel,
@@ -667,7 +673,6 @@
         in_specs=[VMEM] * 2,
         out_specs=[VMEM] * 3,
         scratch_shapes=[
-            table,
             pltpu.SMEM((PLANES, TILE), I32),
             pltpu.SMEM((PLANES, TILE), F32),
             sems,
@@ -685,7 +690,7 @@
         in_specs=[VMEM] * 6,
         out_specs=VMEM,
         scratch_shapes=[
-            table,
+            pltpu.VMEM((near * 4 * PLANES, TILE), F32),
             pltpu.VMEM((PLANES * 8, 8, TILE), F32),
             pltpu.SMEM((PLANES, TILE), I32),
             sems,

time: 86.5 us -> 83.6 us (0.966)
  blocking collectives: 31.6 us -> 52.5 us
  waiting for transfers between devices: 24.3 us -> 12.9 us
  starting transfers between devices: 14.7 us -> 5.62 us
  Pallas kernels: 13.1 us -> 10.2 us
    all_to_all x2 -> x3, blocking collectives: 31.6 us -> 52.5 us  [exchange(): lax.all_to_all(value.reshape(peers, rows, TILE), axes, 0, 0, tiled=True)]
    all_to_all x2 -> x1, waiting for transfers between devices: 24.3 us -> 12.9 us  [exchange(): lax.all_to_all(value.reshape(peers, rows, TILE), axes, 0, 0, tiled=True)]
    all_to_all x2 -> x1, starting transfers between devices: 14.7 us -> 5.62 us  [exchange(): lax.all_to_all(value.reshape(peers, rows, TILE), axes, 0, 0, tiled=True)]
    pallas_call x1, Pallas kernels: 4.52 us -> 2.36 us  [shards(): pl.pallas_call(bin_kernel, out_shape=[f32(near * 4 * PLANES, TILE)] + [f3...]
  transfers between devices with their start and end apart: 2 -> 1, of which waited for: 2 -> 1; matrix products, arithmetic and copies ran while one was open for 0% -> 0% of each run, Pallas kernels for 0% -> 0%
where the time goes in v4:
time: 83.6 us; the launch traced here: 83.4 us
  blocking collectives  52.5 us (63%)
  waiting for transfers between devices  12.9 us (15%)
  Pallas kernels  10.2 us (12%)
  starting transfers between devices  5.62 us (7%)
  between operations  1.36 us (2%)
    all_to_all x3, blocking collectives, exchange(): lax.all_to_all(value.reshape(peers, rows, TILE), axes, 0, 0, tiled=True)  52.5 us
    all_to_all x1, waiting for transfers between devices, exchange(): lax.all_to_all(value.reshape(peers, rows, TILE), axes, 0, 0, tiled=True)  12.9 us
    all_to_all x1, starting transfers between devices, exchange(): lax.all_to_all(value.reshape(peers, rows, TILE), axes, 0, 0, tiled=True)  5.62 us
    pallas_call x1, Pallas kernels, shards(): pl.pallas_call(scan_kernel, out_shape=f32(peers, TILE), in_specs=[VMEM] *...  3.2 us
    pallas_call x1, Pallas kernels, shards(): pl.pallas_call(bin_kernel, out_shape=[f32(near * 4 * PLANES, TILE)] + [f3...  2.36 us
    pallas_call x1, Pallas kernels, shards(): pl.pallas_call(pack_kernel, out_shape=[f32(PLANES * CHUNK, TILE), f32(8,...  1.77 us
  transfers between devices with their start and end apart: 1, of which 1 were waited for; matrix products, arithmetic and copies ran while one was open for 0% of the time, Pallas kernels for 0%

profile of v4, /device:TPU:1, one launch (start us, length us, event | category | flops | bytes accessed | tf_op | source)
XLA Modules:
  0.0 83.4 jit_solution(16964963767816612475)
XLA Ops:
  0.6 0.0 copy-start.1
  0.6 0.1 pad_add_fusion.me_ref
  0.7 0.0 copy-start.6
  0.7 0.0 copy-start.7
  0.7 0.0 copy-start.4
  0.7 0.0 copy-start.5
  0.7 0.0 copy-start.3
  0.8 0.6 copy-done.1
  1.4 0.0 copy-done.6
  1.4 0.0 copy-done.7
  1.4 0.0 copy-done.4
  1.4 0.0 copy-done.5
  1.5 0.0 copy-done.3
  1.5 1.8 %pack_tiles.1 = (f32[384,128]{1,0:T(8,128)S(1)}, f32[8,128]{1,0:T(8,128)S(1)}) custom-call(s32[2,32]{1,0:T(2,128)S(1)} %copy-done.3, f32[2,4]{1,0:T(2,128)S(1)} %copy-done.4, f32[2,4]{1,0:T(2,128)S(1)} %copy-done.5, f32[2,4]{1,0:T(2,128)S(1)} %copy-done.6, s32[64,128]{1,0:T(8,128)S(1)} %bitcast.86, f32[64,128]{1,0:T(8,128)} %bitcast.88, s32[2,64]{1,0:T(2,128)S(1)} %bitcast.91), custom_call_target="tpu_custom_call" | custom-call | tf_op jit(solution)/shard_map/pack_tiles/pallas_call | solution.py:645
  3.3 17.8 %all_to_all.35 = f32[8,48,128]{2,1,0:T(8,128)S(1)} all-to-all(f32[8,48,128]{2,1,0:T(8,128)S(1)} %bitcast.79), channel_id=1, replica_groups=mesh['tm'=4,'z'=8,'x'=4,'core'=2] {'z'}, dimensions={0} | all-to-all | bytes 393216 | tf_op jit(solution)/shard_map/all_to_all | solution.py:575
  21.1 2.4 %bin_tiles.1 = (f32[1024,128]{1,0:T(8,128)S(1)}, f32[192,128]{1,0:T(8,128)S(1)}, f32[192,128]{1,0:T(8,128)S(1)}) custom-call(f32[384,128]{1,0:T(8,128)S(1)} %bitcast.74, s32[8,128]{1,0:T(8,128)S(1)} %fusion.3.name_ref), custom_call_target="tpu_custom_call" | custom-call | tf_op jit(solution)/shard_map/bin_tiles/pallas_call | solution.py:670
  23.4 0.0 copy-start
  23.5 20.9 %all_to_all.36.in_ref = f32[32,32,128]{2,1,0:T(8,128)S(1)} all-to-all(f32[32,32,128]{2,1,0:T(8,128)S(1)} %bitcast.77), channel_id=1, replica_groups=mesh['tm'=4,'z'=8,'x'=4,'core'=2] {'tm','x','core'}, dimensions={0} | all-to-all | bytes 1048576 | tf_op jit(solution)/shard_map/all_to_all | solution.py:575
  44.3 0.0 copy-done
  44.3 1.2 %own_kernel.1 = f32[32,24,128]{2,1,0:T(8,128)S(1)} custom-call(s32[3]{0:T(128)S(1)} %pad_add_fusion.me_ref, f32[32,32,128]{2,1,0:T(8,128)S(1)} %all_to_all.36.in_ref, f32[6,48,256]{2,1,0:T(8,128)S(1)} %bitcast.82), custom_call_target="tpu_custom_call" | custom-call | tf_op jit(solution)/shard_map/own_kernel/pallas_call | solution.py:618
  45.6 13.8 %all_to_all.37 = f32[32,24,128]{2,1,0:T(8,128)S(1)} all-to-all(f32[32,24,128]{2,1,0:T(8,128)S(1)} %own_kernel.1), channel_id=1, replica_groups=mesh['tm'=4,'z'=8,'x'=4,'core'=2] {'tm','x','core'}, dimensions={0} | all-to-all | bytes 786432 | tf_op jit(solution)/shard_map/all_to_all | solution.py:575
  59.3 3.2 %scan_tiles.1 = f32[256,128]{1,0:T(8,128)} custom-call(f32[384,128]{1,0:T(8,128)S(1)} %bitcast.75, s32[8,128]{1,0:T(8,128)S(1)} %fusion.3.name_ref, f32[192,128]{1,0:T(8,128)S(1)} %get-tuple-element.50.cos_ref, f32[192,128]{1,0:T(8,128)S(1)} %get-tuple-element.51.sin_ref, f32[768,128]{1,0:T(8,128)S(1)} %bitcast.76, f32[8,128]{1,0:T(8,128)S(1)} %get-tuple-element.53.own_ref), custom_call_target="tpu_custom_call" | custom-call | tf_op jit(solution)/shard_map/scan_tiles/pallas_call | solution.py:687
  62.5 5.6 %all-to-all-start.6 = ((f32[256,1,128]{2,1,0:T(1,128)}), f32[256,1,128]{2,1,0:T(1,128)S(1)}, u32[]{:S(2)}, u32[]{:S(2)}) async-start(f32[256,1,128]{2,1,0:T(1,128)} %bitcast.26), calls=%async_computation.6 | async-start | bytes 262144 | tf_op jit(solution)/shard_map/all_to_all | solution.py:575
  68.2 12.9 %all-to-all-done.6 = f32[256,1,128]{2,1,0:T(1,128)S(1)} async-done(((f32[256,1,128]{2,1,0:T(1,128)}), f32[256,1,128]{2,1,0:T(1,128)S(1)}, u32[]{:S(2)}, u32[]{:S(2)}) %all-to-all-start.6) | async-done | bytes 131104 | tf_op jit(solution)/shard_map/all_to_all | solution.py:575
  81.1 0.0 copy-start.2
  81.1 1.6 %end_step.1 = (f32[2,4]{1,0:T(2,128)}, f32[2,4]{1,0:T(2,128)}, f32[2,4]{1,0:T(2,128)}, f32[1]{0:T(128)}) custom-call(s32[3]{0:T(128)S(1)} %pad_add_fusion.me_ref, f32[256,128]{1,0:T(8,128)S(1)} %bitcast.78, f32[8,128]{1,0:T(8,128)S(1)} %get-tuple-element.53.own_ref), custom_call_target="tpu_custom_call" | custom-call | tf_op jit(solution)/shard_map/end_step/pallas_call | solution.py:701
  83.4 0.0 copy-done.2
  (3 shorter events, 0.0 us)
Async XLA Ops:
  0.6 0.8 copy-start.1
  0.7 0.7 copy-start.6
  0.7 0.7 copy-start.7
  0.7 0.7 copy-start.4
  0.7 0.7 copy-start.5
  0.7 0.7 copy-start.3
  23.4 20.9 %copy-start = (f32[48,6,256]{2,0,1:T(8,128)S(1)}, f32[48,6,256]{2,0,1:T(8,128)}, u32[]{:S(2)}) copy-start(f32[48,6,256]{2,0,1:T(8,128)} %param.17) | copy-start | bytes 884740
  62.5 18.6 %all-to-all-start.6 = ((f32[256,1,128]{2,1,0:T(1,128)}), f32[256,1,128]{2,1,0:T(1,128)S(1)}, u32[]{:S(2)}, u32[]{:S(2)}) async-start(f32[256,1,128]{2,1,0:T(1,128)} %bitcast.26), calls=%async_computation.6 | async-start | bytes 262144 | tf_op jit(solution)/shard_map/all_to_all | solution.py:575
  81.1 2.3 %copy-start.2 = (f32[2,4096]{1,0:T(2,128)S(1)}, f32[2,4096]{1,0:T(2,128)}, u32[]{:S(2)}) copy-start(f32[2,4096]{1,0:T(2,128)} %param.14) | copy-start | bytes 98308

commit v5 on v4

--- a/solution.py
+++ b/solution.py
@@ -19,9 +19,11 @@
 PER_STEP = 8
 COUNT = 32
 OVER = 33
+HERE = 34
 WAYS = 40
 PLANES = 8
 NEAR = 8
+BINS = 3 * PLANES + 1
 BF16 = jnp.bfloat16
 F32 = jnp.float32
 I32 = jnp.int32
@@ -121,14 +123,20 @@
 
 
 def pack_kernel(*refs):
-    slot_ref, way_ref, res_ref, amp_ref, pix_ref, ang_ref, hits_ref = refs[9:16]
-    out_ref, own_ref = refs[7:9]
-    sems = refs[16]
-    copies = [pltpu.make_async_copy(refs[k], refs[9 + k], sems.at[k]) for k in range(7)]
+    operands, (out_ref, own_ref), kept = refs[:7], refs[7:9], refs[9:16]
+    slot_ref, way_ref, res_ref, amp_ref, pixel_ref, next_ref, sems = refs[16:]
+    pix_ref, ang_ref, hits_ref = kept[4:]
+    targets = kept + (slot_ref, way_ref, res_ref, amp_ref)
+    copies = [
+        pltpu.make_async_copy(operands[k % 7], target, sems.at[k])
+        for k, target in enumerate(targets)
+    ]
     for copy in copies:
         copy.start()
     own_ref[...] = jnp.zeros_like(own_ref)
     out_ref[...] = jnp.zeros_like(out_ref)
+    for z in range(PLANES):
+        next_ref[z] = z * CHUNK
     for copy in copies:
         copy.wait()
     dets, bases = way_ref.shape
@@ -145,39 +153,32 @@
     own_ref[0:1, :] = values
     own_ref[1:2, :] = amps
     sub, lane = iota((PLANES, TILE), 0), iota((PLANES, TILE), 1)
+    at_row = sub * CHUNK + lane
     pix = pix_ref[...]
-    pix_ref[...] = ((pix & 192) << 1) + (pix & 63)
-
-    def tile_step(t, carry):
-        low, high, codes = carry
+    pixel_ref[...] = ((pix & 192) << 1) + (pix & 63)
+
+    def tile_step(t, codes):
         for d in range(dets):
             slot = slot_ref[d, t]
             plane = slot // (2 * NEAR)
-            shift = (plane & 3) * 8
-            upper = plane >> 2
-            place = (jnp.where(upper == 1, high, low) >> shift) & 255
-            one = jnp.left_shift(jnp.int32(1), shift)
-            low = jnp.where(upper == 1, low, low + one)
-            high = jnp.where(upper == 1, high + one, high)
-            place = jnp.minimum(place, ROOM - 1)
+            at = next_ref[plane]
+            next_ref[plane] = at + 1
+            at = jnp.minimum(at, out_ref.shape[0] - ROOM - 1)
             row = t * dets + d
-            at = plane * CHUNK + place
             out_ref[pl.ds(at, 1), :] = ang_ref[pl.ds(row, 1), :]
-            pixels = pix_ref[pl.ds(row, 1), :] + (slot & 1) * 64
+            pixels = pixel_ref[pl.ds(row, 1), :] + (slot & 1) * 64
             out_ref[pl.ds(at + ROOM, 1), :] = pixels.astype(F32)
-            codes = jnp.where((sub == plane) & (lane == place), slot * 64 + row, codes)
-        return low, high, codes
-
-    zero = jnp.int32(0)
-    low, high, codes = lax.fori_loop(
-        0, per_det, tile_step, (zero, zero, jnp.zeros((PLANES, TILE), I32)), unroll=4
-    )
-    over = zero
+            codes = jnp.where(at_row == at, slot * 64 + row, codes)
+        return codes
+
+    codes = lax.fori_loop(0, per_det, tile_step, jnp.zeros((PLANES, TILE), I32), unroll=4)
+    over = jnp.int32(0)
     for z in range(PLANES):
-        count = ((high if z >= 4 else low) >> (8 * (z & 3))) & 255
+        count = next_ref[z] - z * CHUNK
         over = jnp.maximum(over, jnp.where(count > ROOM, 1, 0))
         codes = jnp.where((sub == z) & (lane == COUNT), coded(jnp.minimum(count, ROOM)), codes)
     codes = jnp.where(lane == OVER, coded(over), codes)
+    codes = jnp.where(lane == HERE, coded(sub), codes)
     codes = jnp.where(lane < WAYS, codes.astype(F32), values)
     out_ref[pl.ds(CODES, PLANES, stride=CHUNK), :] = codes
     hits = jnp.concatenate([hits_ref[0:1, :], hits_ref[1:2, :]], axis=1).astype(F32)
@@ -239,8 +240,8 @@
     lax.fori_loop(0, steps, some, 0)
 
 
-def table_rows(q, owner, z):
-    return pl.ds((q * NEAR + owner) * (4 * PLANES) + z, 4, stride=PLANES)
+def table_rows(q, owner, z, chunk, count):
+    return pl.ds((q * NEAR + owner) * chunk + z, count, stride=PLANES)
 
 
 def halves(x):
@@ -254,12 +255,17 @@
         c, s = cos_sin(2.0 * in_ref[z * CHUNK : z * CHUNK + ANGLES, :])
         cos_ref[z * ANGLES : (z + 1) * ANGLES, :] = c
         sin_ref[z * ANGLES : (z + 1) * ANGLES, :] = s
-    hits = in_ref[pl.ds(HITS, PLANES, stride=CHUNK), :]
-    for at in range(0, out_ref.shape[0], PLANES):
-        last = at // PLANES % 4 == 3
-        out_ref[at : at + PLANES, :] = hits if last else jnp.zeros((PLANES, TILE), F32)
+    out_ref[...] = jnp.zeros_like(out_ref)
     for copy in copies:
         copy.wait()
+    hits = in_ref[pl.ds(HITS, PLANES, stride=CHUNK), :].astype(BF16)
+    lane, deep = iota((TILE, TILE), 1), iota((TILE, TILE), 0)
+    here = (lane & 1) * 64 + names[0, HERE] * NEAR + ((lane >> 1) & (NEAR - 1))
+    moved = dot(hits, jnp.where(deep == here, 1.0, 0.0).astype(BF16))
+    moved = jnp.where(iota((PLANES, TILE), 1) >> 4 == iota((PLANES, TILE), 0), moved, 0.0)
+    moved = jnp.sum(moved, axis=0, keepdims=True)
+    for at in range(BINS - 1, out_ref.shape[0], BINS):
+        out_ref[at : at + 1, :] = moved
 
     def use(tiles, hots, weights):
         both = jnp.concatenate([halves(weight) for weight in weights], axis=0)
@@ -269,23 +275,32 @@
             mine = res[32 * n : 32 * n + 32, n * TILE : (n + 1) * TILE]
             mine = (mine[:16] + mine[16:]) * height
             for q in range(4):
-                rows = table_rows(q, owner, z)
-                out_ref[rows, :] = out_ref[rows, :] + mine[4 * q : 4 * q + 4]
+                rows = table_rows(q, owner, z, BINS, 3)
+                out_ref[rows, :] = out_ref[rows, :] + mine[4 * q : 4 * q + 3]
 
     each_pair(in_ref, names, cos_ref, sin_ref, use)
 
 
 def own_kernel(me_ref, in_ref, prec_ref, out_ref):
-    peers = in_ref.shape[0]
+    peers = in_ref.shape[0] // BINS
     sources = peers * PLANES
+    owner = me_ref[0:1, :] & (NEAR - 1)
 
     def take(c):
-        return in_ref[:, c * PLANES : (c + 1) * PLANES, :].reshape(sources, TILE)
+        if c < 3:
+            at = [w * BINS + c * PLANES for w in range(peers)]
+            return jnp.concatenate([in_ref[a : a + PLANES, :] for a in at], axis=0)
+        mine = iota((PLANES, TILE), 1) >> 4 == iota((PLANES, TILE), 0)
+        at = [w * BINS + BINS - 1 for w in range(peers)]
+        return jnp.concatenate([jnp.where(mine, in_ref[a : a + 1, :], 0.0) for a in at], axis=0)
 
     def put(c, value):
         out_ref[:, c * PLANES : (c + 1) * PLANES, :] = value.reshape(peers, PLANES, TILE)
 
-    own_solve(me_ref[0], me_ref[1], sources, take, prec_ref, put)
+    def place(lane, k):
+        return (lane & 15) == 2 * owner + k
+
+    own_solve(place, me_ref[1:2, :], sources, take, prec_ref, put)
 
 
 def slow_own_kernel(me_ref, in_ref, prec_ref, out_ref):
@@ -297,16 +312,19 @@
     def put(c, value):
         out_ref[pl.ds(c, sources, stride=4), :] = value
 
-    own_solve(me_ref[0], me_ref[1], sources, take, prec_ref, put)
+    def place(lane, k):
+        return lane == me_ref[0:1, :] + 64 * k
+
+    own_solve(place, me_ref[1:2, :], sources, take, prec_ref, put)
     put(3, jnp.zeros((sources, TILE), F32))
 
 
-def own_solve(me, quarter, sources, take, prec_ref, put):
+def own_solve(place, quarter, sources, take, prec_ref, put):
     subs = prec_ref.shape[1]
     ids = take(3).astype(BF16)
     lane = iota((16, TILE), 1)
     row = iota((16, TILE), 0)
-    pick = jnp.where((lane == me + 64 * row) & (row < 2), 1.0, 0.0).astype(BF16)
+    pick = jnp.where(place(lane, row) & (row < 2), 1.0, 0.0).astype(BF16)
     id_rows = dot(pick, ids, NT).astype(I32)
     sub = iota((subs, sources), 0)
     hot = jnp.concatenate(
@@ -325,8 +343,9 @@
         res = jnp.where(left, res[:subs], res[subs:])
         binned.append(res + pltpu.roll(res, 64, 1))
 
-    block = quarter // 2
-    keep = left == ((quarter % 2) == 0)
+    quarter = jnp.broadcast_to(quarter, (subs, TILE))
+    keep = (iota((subs, TILE), 1) >> 6) == (quarter & 1)
+    block = quarter >> 1
     prec = []
     for e in range(6):
         value = jnp.where(block == 0, prec_ref[e, :, :TILE], prec_ref[e, :, TILE:])
@@ -339,7 +358,7 @@
     ]
 
     deep, wide = iota((TILE, TILE), 0), iota((TILE, TILE), 1)
-    spread = jnp.where(deep == me + (wide & 64), 1.0, 0.0).astype(BF16)
+    spread = jnp.where(place(deep, wide >> 6), 1.0, 0.0).astype(BF16)
     named = dot(ids, spread).astype(I32)
     back = jnp.where(named == (iota((sources, TILE), 1) & 63), 1.0, 0.0).astype(BF16)
     back = jnp.concatenate([back, back], axis=1)
@@ -369,7 +388,7 @@
     def use(tiles, hots, weights):
         both = []
         for z, owner, _, _ in tiles:
-            value = [sky_ref[table_rows(q, owner, z), :] for q in range(4)]
+            value = [sky_ref[table_rows(q, owner, z, 4 * PLANES, 4), :] for q in range(4)]
             both.append(halves(jnp.concatenate(value, axis=0)))
         res = dot(jnp.concatenate(both, axis=0), jnp.concatenate(hots, axis=1))
         for n, (z, _, base, valid) in enumerate(tiles):
@@ -393,7 +412,7 @@
     out_ref[...] = jnp.broadcast_to(row, out_ref.shape)
 
 
-def end_kernel(me_ref, in_ref, own_ref, amp_out, res_out, dir_out, over_out, keep_ref):
+def end_kernel(me_ref, in_ref, own_ref, amp_out, res_out, dir_out, over_out):
     dets, bases = amp_out.shape
     spans = in_ref.shape[0] // (PLANES * NEAR)
     lane = iota((NEAR, TILE), 1)
@@ -414,7 +433,7 @@
         scan.append(a)
         way.append(w)
         rest.append(r)
-    over = jnp.max(jnp.where(lane == 96, over, 0.0))
+    over = jnp.where(lane == 96, over, 0.0)
     zero = jnp.zeros((NEAR, TILE), F32)
     applied = []
     for i in range(spans):
@@ -435,10 +454,16 @@
     factor = now / total([w * a for w, a in zip(way, applied)])
     fresh = [r - factor * a for r, a in zip(rest, applied)]
     ratio = total([f * f for f in fresh]) / now
+    sub = iota((NEAR, TILE), 0)
+    det = jnp.broadcast_to(me_ref[0:1, :], (NEAR, TILE))
+    span = jnp.broadcast_to(me_ref[1:2, :], (NEAR, TILE))
+    here = (sub == (det & (NEAR - 1))) & ((lane >> 3) == (det >> 3))
+    mine = zero
     for i in range(spans):
-        keep_ref[i * NEAR : (i + 1) * NEAR, :] = fresh[i]
-    mine = jnp.broadcast_to(keep_ref[pl.ds(me_ref[1] * NEAR + me_ref[0] % NEAR, 1), :], (8, TILE))
-    mine = pltpu.roll(mine, (TILE - (me_ref[0] // NEAR) * 8) % TILE, 1)[0:1]
+        mine = mine + jnp.where(here & (span == i), fresh[i], 0.0)
+    for shift in (64, 32, 16, 8):
+        mine = mine + pltpu.roll(mine, shift, 1)
+    mine = jnp.sum(mine, axis=0, keepdims=True)
     my_way = own_ref[0:1, 72:80]
     my_fresh = mine[:, 0:8]
     moved = own_ref[1:2, 0:8] + factor * my_way
@@ -448,7 +473,7 @@
         amp_out[d : d + 1, :] = moved[:, lo:hi]
         res_out[d : d + 1, :] = my_fresh[:, lo:hi]
         dir_out[d : d + 1, :] = turn[:, lo:hi]
-    over_out[0] = over
+    over_out[0] = jnp.max(over)
 
 
 def slow_bin_kernel(slot_ref, dir_ref, pix_ref, ang_ref, hits_ref, out_ref, cos_ref, sin_ref, acc_ref):
@@ -571,6 +596,9 @@
 
 
 def exchange(value, axes, rows):
+    if rows % 4:
+        moved = lax.all_to_all(value.reshape(-1, 1, TILE), axes, 0, 0, tiled=True)
+        return moved.reshape(value.shape)
     peers = value.shape[0] // rows
     moved = lax.all_to_all(value.reshape(peers, rows, TILE), axes, 0, 0, tiled=True)
     return moved.reshape(value.shape)
@@ -580,7 +608,7 @@
     return jax.ShapeDtypeStruct(shape, F32)
 
 
-def slow(me, amp, res, way, pix, ang, places, hits, prec):
+def slow(spot, me, prec, places, way, res, amp, pix, ang, hits):
     tiles = pix.shape[0]
     slots = hits.shape[1] * 2
     peers = 4 * hits.shape[1]
@@ -610,7 +638,7 @@
         out_specs=[VMEM] * 3,
         scratch_shapes=[pltpu.VMEM((2, peers, TILE), F32)],
         name="slow_end",
-    )(me, exchange(last, ALL, 1), amp)
+    )(spot, exchange(last, ALL, 1), amp)
 
 
 def solve(kernel, args, *shape):
@@ -618,7 +646,7 @@
     return pl.pallas_call(
         kernel,
         out_shape=f32(*shape),
-        in_specs=[SMEM, VMEM, VMEM],
+        in_specs=[VMEM] * 3,
         out_specs=VMEM,
         compiler_params=SMALL,
         name=kernel.__name__,
@@ -639,27 +667,27 @@
     pix, ang = rows_of(pix), rows_of(ang)
     hits = hits.reshape(owners, 2).T
     prec = prec.transpose(1, 0, 2)
-    me = jnp.stack([lax.axis_index(DET), lax.axis_index("tm"), owners]).astype(I32)
+    spot = jnp.stack([lax.axis_index(DET), lax.axis_index("tm"), owners]).astype(I32)
+    me = jnp.broadcast_to(jnp.pad(spot, (0, 5))[:, None], (8, TILE))
 
     me, places = lax.optimization_barrier((me, places))
-    packed, own = pl.pallas_call(
+    given = (places, way, res, amp, pix, ang, hits)
+    given = tuple(pltpu.with_memory_space_constraint(v, pltpu.HBM) for v in given)
+    packed, own, *given = pl.pallas_call(
         pack_kernel,
-        out_shape=[f32(PLANES * CHUNK, TILE), f32(8, TILE)],
+        out_shape=[f32(PLANES * CHUNK, TILE), f32(8, TILE)]
+        + [jax.ShapeDtypeStruct(v.shape, v.dtype) for v in given],
         in_specs=[pl.BlockSpec(memory_space=pltpu.HBM)] * 7,
-        out_specs=[VMEM, VMEM],
-        scratch_shapes=[
-            pltpu.SMEM(places.shape, I32),
-            pltpu.SMEM(way.shape, F32),
-            pltpu.SMEM(way.shape, F32),
-            pltpu.SMEM(way.shape, F32),
+        out_specs=[VMEM] * 9,
+        scratch_shapes=[pltpu.SMEM(v.shape, v.dtype) for v in given[:4]]
+        + [
             pltpu.VMEM((tiles, TILE), I32),
-            pltpu.VMEM((tiles, TILE), F32),
-            pltpu.VMEM(hits.shape, I32),
-            pltpu.SemaphoreType.DMA((7,)),
+            pltpu.SMEM((PLANES,), I32),
+            pltpu.SemaphoreType.DMA((11,)),
         ],
         compiler_params=SMALL,
         name="pack_tiles",
-    )(places, way, res, amp, pix, ang, hits)
+    )(*given)
     packed = exchange(packed, "z", CHUNK)
 
     raw = packed.reshape(PLANES, CHUNK, TILE)[:, CODES].astype(I32)
@@ -669,7 +697,7 @@
     sems = pltpu.SemaphoreType.DMA((PLANES + 1,))
     binned, cosine, sine = pl.pallas_call(
         bin_kernel,
-        out_shape=[f32(near * 4 * PLANES, TILE)] + [f32(PLANES * ANGLES, TILE)] * 2,
+        out_shape=[f32(near * BINS, TILE)] + [f32(PLANES * ANGLES, TILE)] * 2,
         in_specs=[VMEM] * 2,
         out_specs=[VMEM] * 3,
         scratch_shapes=[
@@ -680,7 +708,7 @@
         compiler_params=SMALL,
         name="bin_tiles",
     )(packed, names)
-    binned = exchange(binned, PLANE, 4 * PLANES).reshape(near, 4 * PLANES, TILE)
+    binned = exchange(binned, PLANE, BINS)
     sky = solve(own_kernel, (me, binned, prec), near, 3 * PLANES)
     sky = exchange(sky.reshape(near * 3 * PLANES, TILE), PLANE, 3 * PLANES)
 
@@ -701,15 +729,15 @@
     *out, over = pl.pallas_call(
         end_kernel,
         out_shape=[f32(*amp.shape)] * 3 + [f32(1)],
-        in_specs=[SMEM, VMEM, VMEM],
+        in_specs=[VMEM] * 3,
         out_specs=[VMEM] * 3 + [SMEM],
-        scratch_shapes=[pltpu.VMEM((4 * NEAR, TILE), F32)],
         compiler_params=SMALL,
         name="end_step",
     )(me, exchange(last, ALL, 1), own)
+    over, *given = lax.optimization_barrier((over, *given))
     return lax.cond(
         over[0] > 0,
-        lambda: tuple(slow(me, amp, res, way, pix, ang, places, hits, prec)),
+        lambda: tuple(slow(spot, me, prec, *given)),
         lambda: tuple(out),
     )
 

time: 83.6 us -> 79 us (0.945)
  blocking collectives: 52.5 us -> 68.5 us
  waiting for transfers between devices: 12.9 us -> 0 us
  starting transfers between devices: 5.62 us -> 0 us
  Pallas kernels: 10.2 us -> 8.57 us
    all_to_all x0 -> x2, blocking collectives: none -> 37 us  [exchange(): moved = lax.all_to_all(value.reshape(-1, 1, TILE), axes, 0, 0, tiled=True)]
    all_to_all x3 -> x2, blocking collectives: 52.5 us -> 31.5 us  [exchange(): lax.all_to_all(value.reshape(peers, rows, TILE), axes, 0, 0, tiled=True)]
    all_to_all x1 -> x0, waiting for transfers between devices: 12.9 us -> none  [exchange(): lax.all_to_all(value.reshape(peers, rows, TILE), axes, 0, 0, tiled=True)]
    all_to_all x1 -> x0, starting transfers between devices: 5.62 us -> none  [exchange(): lax.all_to_all(value.reshape(peers, rows, TILE), axes, 0, 0, tiled=True)]
  transfers between devices with their start and end apart: 1 -> 0, of which waited for: 1 -> 0; matrix products, arithmetic and copies ran while one was open for 0% -> 0% of each run, Pallas kernels for 0% -> 0%
where the time goes in v5:
time: 79 us; the launch traced here: 78.5 us
  blocking collectives  68.5 us (87%)
  Pallas kernels  8.57 us (11%)
  between operations  1.25 us (2%)
    all_to_all x2, blocking collectives, exchange(): moved = lax.all_to_all(value.reshape(-1, 1, TILE), axes, 0, 0, tiled=True)  37 us
    all_to_all x2, blocking collectives, exchange(): lax.all_to_all(value.reshape(peers, rows, TILE), axes, 0, 0, tiled=True)  31.5 us
    pallas_call x1, Pallas kernels, shards(): pl.pallas_call(scan_kernel, out_shape=f32(peers, TILE), in_specs=[VMEM] *...  2.56 us
    pallas_call x1, Pallas kernels, shards(): pl.pallas_call(bin_kernel, out_shape=[f32(near * BINS, TILE)] + [f32(PLAN...  2.47 us
    pallas_call x1, Pallas kernels, shards(): pl.pallas_call(pack_kernel, out_shape=[f32(PLANES * CHUNK, TILE), f32(8,...  1.64 us

profile of v5, /device:TPU:1, one launch (start us, length us, event | category | flops | bytes accessed | tf_op | source)
XLA Modules:
  0.0 78.5 jit_solution(14577253914340969372)
XLA Ops:
  0.6 0.1 pad_add_fusion
  0.7 0.1 broadcast_in_dim.2.me_ref
  0.8 1.6 %pack_tiles.1 = (f32[384,128]{1,0:T(8,128)S(1)}, f32[8,128]{1,0:T(8,128)S(1)}, s32[2,32]{1,0:T(2,128)S(1)}, f32[2,4]{1,0:T(2,128)S(1)}, f32[2,4]{1,0:T(2,128)S(1...) custom-call(s32[2,32]{1,0:T(2,128)} %refs_0_, f32[2,4]{1,0:T(2,128)} %refs_1_.1, ...), custom_call_target="tpu_custom_call" | custom-call | tf_op jit(solution)/shard_map/pack_tiles/pallas_call | solution.py:676
  2.4 17.8 %all_to_all.35 = f32[8,48,128]{2,1,0:T(8,128)S(1)} all-to-all(f32[8,48,128]{2,1,0:T(8,128)S(1)} %bitcast.84), channel_id=1, replica_groups=mesh['tm'=4,'z'=8,'x'=4,'core'=2] {'z'}, dimensions={0} | all-to-all | bytes 393216 | tf_op jit(solution)/shard_map/all_to_all | solution.py:603
  20.3 2.5 %bin_tiles.1 = (f32[800,128]{1,0:T(8,128)S(1)}, f32[192,128]{1,0:T(8,128)S(1)}, f32[192,128]{1,0:T(8,128)S(1)}) custom-call(f32[384,128]{1,0:T(8,128)S(1)} %bitcast.77, s32[8,128]{1,0:T(8,128)S(1)} %fusion.3.name_ref), custom_call_target="tpu_custom_call" | custom-call | tf_op jit(solution)/shard_map/bin_tiles/pallas_call | solution.py:698
  22.7 0.0 copy-start
  22.8 19.4 %all_to_all.36 = f32[800,1,128]{2,1,0:T(1,128)S(1)} all-to-all(f32[800,1,128]{2,1,0:T(1,128)S(1)} %bitcast.83), channel_id=1, replica_groups=mesh['tm'=4,'z'=8,'x'=4,'core'=2] {'tm','x','core'}, dimensions={0} | all-to-all | bytes 819200 | tf_op jit(solution)/shard_map/all_to_all | solution.py:600
  42.2 0.0 copy-done
  42.2 0.7 own_kernel.1
  42.9 13.7 %all_to_all.37 = f32[32,24,128]{2,1,0:T(8,128)S(1)} all-to-all(f32[32,24,128]{2,1,0:T(8,128)S(1)} %own_kernel.1), channel_id=1, replica_groups=mesh['tm'=4,'z'=8,'x'=4,'core'=2] {'tm','x','core'}, dimensions={0} | all-to-all | bytes 786432 | tf_op jit(solution)/shard_map/all_to_all | solution.py:603
  56.5 2.6 %scan_tiles.1 = f32[256,128]{1,0:T(8,128)S(1)} custom-call(f32[384,128]{1,0:T(8,128)S(1)} %bitcast.78, s32[8,128]{1,0:T(8,128)S(1)} %fusion.3.name_ref, f32[192,128]{1,0:T(8,128)S(1)} %get-tuple-element.68.cos_ref, f32[192,128]{1,0:T(8,128)S(1)} %get-tuple-element.69.sin_ref, f32[768,128]{1,0:T(8,128)S(1)} %bitcast.80, f32[8,128]{1,0:T(8,128)S(1)} %get-tuple-element.71.own_ref), custom_call_target="tpu_custom_call" | custom-call | tf_op jit(solution)/shard_map/scan_tiles/pallas_call | solution.py:715
  59.1 17.6 %all_to_all.38 = f32[256,1,128]{2,1,0:T(1,128)S(1)} all-to-all(f32[256,1,128]{2,1,0:T(1,128)S(1)} %bitcast.81), channel_id=1, replica_groups=mesh['tm'=4,'z'=8,'x'=4,'core'=2] {'tm','z','x','core'}, dimensions={0} | all-to-all | bytes 262144 | tf_op jit(solution)/shard_map/all_to_all | solution.py:600
  76.7 1.2 %end_step.1 = (f32[2,4]{1,0:T(2,128)}, f32[2,4]{1,0:T(2,128)}, f32[2,4]{1,0:T(2,128)}, f32[1]{0:T(128)}) custom-call(s32[8,128]{1,0:T(8,128)S(1)} %broadcast_in_dim.2.me_ref, f32[256,128]{1,0:T(8,128)S(1)} %bitcast.82, f32[8,128]{1,0:T(8,128)S(1)} %get-tuple-element.71.own_ref), custom_call_target="tpu_custom_call" | custom-call | tf_op jit(solution)/shard_map/end_step/pallas_call | solution.py:729
  (4 shorter events, 0.0 us)
Async XLA Ops:
  22.7 19.5 %copy-start = (f32[48,6,256]{2,0,1:T(8,128)S(1)}, f32[48,6,256]{2,0,1:T(8,128)}, u32[]{:S(2)}) copy-start(f32[48,6,256]{2,0,1:T(8,128)} %param.17) | copy-start | bytes 884740

commit v6 on v5

--- a/solution.py
+++ b/solution.py
@@ -16,7 +16,7 @@
 HITS = 2 * ROOM + 1
 ANGLES = 24
 GROUP = 4
-PER_STEP = 8
+PER_STEP = 10
 COUNT = 32
 OVER = 33
 HERE = 34
@@ -394,12 +394,16 @@
         for n, (z, _, base, valid) in enumerate(tiles):
             mine = res[32 * n : 32 * n + 32, n * TILE : (n + 1) * TILE]
             mine = (mine[:16] + mine[16:]) * weights[n]
-            at = z * 8 + base
-            sum_ref[at] = sum_ref[at] + (mine[:8] + mine[8:]) * jnp.where(valid, 1.0, 0.0)
+            rows = pl.ds(pl.multiple_of((z * 8 + base) * 8, 8), 8)
+            mine = (mine[:8] + mine[8:]) * jnp.where(valid, 1.0, 0.0)
+            sum_ref[rows, :] = sum_ref[rows, :] + mine
 
     each_pair(in_ref, names, cos_ref, sin_ref, use)
     count = PLANES * 8
-    sums = jnp.sum(jnp.sum(sum_ref[...], axis=1), axis=1, keepdims=True)
+    sums = sum_ref[pl.ds(0, count, stride=8), :]
+    for k in range(1, 8):
+        sums = sums + sum_ref[pl.ds(k, count, stride=8), :]
+    sums = jnp.sum(sums, axis=1, keepdims=True)
     lane, sub = iota((count, TILE), 1), iota((count, TILE), 0)
     row = jnp.sum(jnp.where(lane == sub, sums, 0.0), axis=0, keepdims=True)
     row = row * np.float32(1.0 / 1024)
@@ -608,7 +612,8 @@
     return jax.ShapeDtypeStruct(shape, F32)
 
 
-def slow(spot, me, prec, places, way, res, amp, pix, ang, hits):
+def slow(owners, me, prec, places, way, res, amp, pix, ang, hits):
+    spot = jnp.stack([me[0, 0], me[1, 0], jnp.int32(owners)])
     tiles = pix.shape[0]
     slots = hits.shape[1] * 2
     peers = 4 * hits.shape[1]
@@ -667,8 +672,8 @@
     pix, ang = rows_of(pix), rows_of(ang)
     hits = hits.reshape(owners, 2).T
     prec = prec.transpose(1, 0, 2)
-    spot = jnp.stack([lax.axis_index(DET), lax.axis_index("tm"), owners]).astype(I32)
-    me = jnp.broadcast_to(jnp.pad(spot, (0, 5))[:, None], (8, TILE))
+    first = lax.broadcasted_iota(I32, (8, TILE), 0) == 0
+    me = jnp.where(first, lax.axis_index(DET), lax.axis_index("tm")).astype(I32)
 
     me, places = lax.optimization_barrier((me, places))
     given = (places, way, res, amp, pix, ang, hits)
@@ -719,7 +724,7 @@
         out_specs=VMEM,
         scratch_shapes=[
             pltpu.VMEM((near * 4 * PLANES, TILE), F32),
-            pltpu.VMEM((PLANES * 8, 8, TILE), F32),
+            pltpu.VMEM((PLANES * 64, TILE), F32),
             pltpu.SMEM((PLANES, TILE), I32),
             sems,
         ],
@@ -737,7 +742,7 @@
     over, *given = lax.optimization_barrier((over, *given))
     return lax.cond(
         over[0] > 0,
-        lambda: tuple(slow(spot, me, prec, *given)),
+        lambda: tuple(slow(owners, me, prec, *given)),
         lambda: tuple(out),
     )
 

time: 79 us -> 79 us (level)
  no operation moved by 1% of the time
where the time goes in v6:
time: 79 us; the launch traced here: 78.5 us
  blocking collectives  68.8 us (87%)
  Pallas kernels  8.26 us (10%)
  between operations  1.32 us (2%)
    all_to_all x2, blocking collectives, exchange(): moved = lax.all_to_all(value.reshape(-1, 1, TILE), axes, 0, 0, tiled=True)  37.3 us
    all_to_all x2, blocking collectives, exchange(): lax.all_to_all(value.reshape(peers, rows, TILE), axes, 0, 0, tiled=True)  31.5 us
    pallas_call x1, Pallas kernels, shards(): pl.pallas_call(scan_kernel, out_shape=f32(peers, TILE), in_specs=[VMEM] *...  2.42 us
    pallas_call x1, Pallas kernels, shards(): pl.pallas_call(bin_kernel, out_shape=[f32(near * BINS, TILE)] + [f32(PLAN...  2.3 us
    pallas_call x1, Pallas kernels, shards(): pl.pallas_call(pack_kernel, out_shape=[f32(PLANES * CHUNK, TILE), f32(8,...  1.64 us

profile of v6, /device:TPU:1, one launch (start us, length us, event | category | flops | bytes accessed | tf_op | source)
XLA Modules:
  0.0 78.5 jit_solution(1266046952693965997)
XLA Ops:
  0.6 0.1 iota.7.me_ref
  0.7 1.6 %pack_tiles.1 = (f32[384,128]{1,0:T(8,128)S(1)}, f32[8,128]{1,0:T(8,128)S(1)}, s32[2,32]{1,0:T(2,128)S(1)}, f32[2,4]{1,0:T(2,128)S(1)}, f32[2,4]{1,0:T(2,128)S(1...) custom-call(s32[2,32]{1,0:T(2,128)} %refs_0_, f32[2,4]{1,0:T(2,128)} %refs_1_.1, ...), custom_call_target="tpu_custom_call" | custom-call | tf_op jit(solution)/shard_map/pack_tiles/pallas_call | solution.py:681
  2.4 17.8 %all_to_all.34 = f32[8,48,128]{2,1,0:T(8,128)S(1)} all-to-all(f32[8,48,128]{2,1,0:T(8,128)S(1)} %bitcast.84), channel_id=1, replica_groups=mesh['tm'=4,'z'=8,'x'=4,'core'=2] {'z'}, dimensions={0} | all-to-all | bytes 393216 | tf_op jit(solution)/shard_map/all_to_all | solution.py:607
  20.2 2.3 %bin_tiles.1 = (f32[800,128]{1,0:T(8,128)S(1)}, f32[192,128]{1,0:T(8,128)S(1)}, f32[192,128]{1,0:T(8,128)S(1)}) custom-call(f32[384,128]{1,0:T(8,128)S(1)} %bitcast.77, s32[8,128]{1,0:T(8,128)S(1)} %fusion.3.name_ref), custom_call_target="tpu_custom_call" | custom-call | tf_op jit(solution)/shard_map/bin_tiles/pallas_call | solution.py:703
  22.5 0.0 copy-start
  22.5 19.8 %all_to_all.35 = f32[800,1,128]{2,1,0:T(1,128)S(1)} all-to-all(f32[800,1,128]{2,1,0:T(1,128)S(1)} %bitcast.83), channel_id=1, replica_groups=mesh['tm'=4,'z'=8,'x'=4,'core'=2] {'tm','x','core'}, dimensions={0} | all-to-all | bytes 819200 | tf_op jit(solution)/shard_map/all_to_all | solution.py:604
  42.3 0.0 copy-done
  42.3 0.7 own_kernel.1
  43.0 13.7 %all_to_all.36 = f32[32,24,128]{2,1,0:T(8,128)S(1)} all-to-all(f32[32,24,128]{2,1,0:T(8,128)S(1)} %own_kernel.1), channel_id=1, replica_groups=mesh['tm'=4,'z'=8,'x'=4,'core'=2] {'tm','x','core'}, dimensions={0} | all-to-all | bytes 786432 | tf_op jit(solution)/shard_map/all_to_all | solution.py:607
  56.6 2.4 %scan_tiles.1 = f32[256,128]{1,0:T(8,128)S(1)} custom-call(f32[384,128]{1,0:T(8,128)S(1)} %bitcast.78, s32[8,128]{1,0:T(8,128)S(1)} %fusion.3.name_ref, f32[192,128]{1,0:T(8,128)S(1)} %get-tuple-element.65.cos_ref, f32[192,128]{1,0:T(8,128)S(1)} %get-tuple-element.66.sin_ref, f32[768,128]{1,0:T(8,128)S(1)} %bitcast.80, f32[8,128]{1,0:T(8,128)S(1)} %get-tuple-element.68.own_ref), custom_call_target="tpu_custom_call" | custom-call | tf_op jit(solution)/shard_map/scan_tiles/pallas_call | solution.py:720
  59.0 17.5 %all_to_all.37 = f32[256,1,128]{2,1,0:T(1,128)S(1)} all-to-all(f32[256,1,128]{2,1,0:T(1,128)S(1)} %bitcast.81), channel_id=1, replica_groups=mesh['tm'=4,'z'=8,'x'=4,'core'=2] {'tm','z','x','core'}, dimensions={0} | all-to-all | bytes 262144 | tf_op jit(solution)/shard_map/all_to_all | solution.py:604
  76.6 1.2 %end_step.1 = (f32[2,4]{1,0:T(2,128)}, f32[2,4]{1,0:T(2,128)}, f32[2,4]{1,0:T(2,128)}, f32[1]{0:T(128)}) custom-call(s32[8,128]{1,0:T(8,128)S(1)} %iota.7.me_ref, f32[256,128]{1,0:T(8,128)S(1)} %bitcast.82, f32[8,128]{1,0:T(8,128)S(1)} %get-tuple-element.68.own_ref), custom_call_target="tpu_custom_call" | custom-call | tf_op jit(solution)/shard_map/end_step/pallas_call | solution.py:734
  (4 shorter events, 0.0 us)
Async XLA Ops:
  22.5 19.8 %copy-start = (f32[48,6,256]{2,0,1:T(8,128)S(1)}, f32[48,6,256]{2,0,1:T(8,128)}, u32[]{:S(2)}) copy-start(f32[48,6,256]{2,0,1:T(8,128)} %param.17) | copy-start | bytes 884740

commit v7 on v6

--- a/solution.py
+++ b/solution.py
@@ -16,7 +16,7 @@
 HITS = 2 * ROOM + 1
 ANGLES = 24
 GROUP = 4
-PER_STEP = 10
+PER_STEP = 12
 COUNT = 32
 OVER = 33
 HERE = 34

time: 79 us -> 79.2 us (level)
  blocking collectives: 68.8 us -> 69.7 us
    all_to_all x2, blocking collectives: 37.3 us -> 38.3 us  [exchange(): moved = lax.all_to_all(value.reshape(-1, 1, TILE), axes, 0, 0, tiled=True)]
where the time goes in v7:
time: 79.2 us; the launch traced here: 79 us
  blocking collectives  69.7 us (88%)
  Pallas kernels  7.85 us (10%)
  between operations  1.32 us (2%)
    all_to_all x2, blocking collectives, exchange(): moved = lax.all_to_all(value.reshape(-1, 1, TILE), axes, 0, 0, tiled=True)  38.3 us
    all_to_all x2, blocking collectives, exchange(): lax.all_to_all(value.reshape(peers, rows, TILE), axes, 0, 0, tiled=True)  31.4 us
    pallas_call x1, Pallas kernels, shards(): pl.pallas_call(scan_kernel, out_shape=f32(peers, TILE), in_specs=[VMEM] *...  2.2 us
    pallas_call x1, Pallas kernels, shards(): pl.pallas_call(bin_kernel, out_shape=[f32(near * BINS, TILE)] + [f32(PLAN...  2.11 us
    pallas_call x1, Pallas kernels, shards(): pl.pallas_call(pack_kernel, out_shape=[f32(PLANES * CHUNK, TILE), f32(8,...  1.64 us

profile of v7, /device:TPU:1, one launch (start us, length us, event | category | flops | bytes accessed | tf_op | source)
XLA Modules:
  0.0 79.0 jit_solution(243452723635913858)
XLA Ops:
  0.6 0.1 iota.7.me_ref
  0.7 1.6 %pack_tiles.1 = (f32[384,128]{1,0:T(8,128)S(1)}, f32[8,128]{1,0:T(8,128)S(1)}, s32[2,32]{1,0:T(2,128)S(1)}, f32[2,4]{1,0:T(2,128)S(1)}, f32[2,4]{1,0:T(2,128)S(1...) custom-call(s32[2,32]{1,0:T(2,128)} %refs_0_, f32[2,4]{1,0:T(2,128)} %refs_1_.1, ...), custom_call_target="tpu_custom_call" | custom-call | tf_op jit(solution)/shard_map/pack_tiles/pallas_call | solution.py:681
  2.4 17.8 %all_to_all.34 = f32[8,48,128]{2,1,0:T(8,128)S(1)} all-to-all(f32[8,48,128]{2,1,0:T(8,128)S(1)} %bitcast.84), channel_id=1, replica_groups=mesh['tm'=4,'z'=8,'x'=4,'core'=2] {'z'}, dimensions={0} | all-to-all | bytes 393216 | tf_op jit(solution)/shard_map/all_to_all | solution.py:607
  20.2 2.1 %bin_tiles.1 = (f32[800,128]{1,0:T(8,128)S(1)}, f32[192,128]{1,0:T(8,128)S(1)}, f32[192,128]{1,0:T(8,128)S(1)}) custom-call(f32[384,128]{1,0:T(8,128)S(1)} %bitcast.77, s32[8,128]{1,0:T(8,128)S(1)} %fusion.3.name_ref), custom_call_target="tpu_custom_call" | custom-call | tf_op jit(solution)/shard_map/bin_tiles/pallas_call | solution.py:703
  22.3 0.0 copy-start
  22.3 19.9 %all_to_all.35 = f32[800,1,128]{2,1,0:T(1,128)S(1)} all-to-all(f32[800,1,128]{2,1,0:T(1,128)S(1)} %bitcast.83), channel_id=1, replica_groups=mesh['tm'=4,'z'=8,'x'=4,'core'=2] {'tm','x','core'}, dimensions={0} | all-to-all | bytes 819200 | tf_op jit(solution)/shard_map/all_to_all | solution.py:604
  42.2 0.0 copy-done
  42.2 0.7 own_kernel.1
  42.9 13.7 %all_to_all.36 = f32[32,24,128]{2,1,0:T(8,128)S(1)} all-to-all(f32[32,24,128]{2,1,0:T(8,128)S(1)} %own_kernel.1), channel_id=1, replica_groups=mesh['tm'=4,'z'=8,'x'=4,'core'=2] {'tm','x','core'}, dimensions={0} | all-to-all | bytes 786432 | tf_op jit(solution)/shard_map/all_to_all | solution.py:607
  56.6 2.2 %scan_tiles.1 = f32[256,128]{1,0:T(8,128)S(1)} custom-call(f32[384,128]{1,0:T(8,128)S(1)} %bitcast.78, s32[8,128]{1,0:T(8,128)S(1)} %fusion.3.name_ref, f32[192,128]{1,0:T(8,128)S(1)} %get-tuple-element.65.cos_ref, f32[192,128]{1,0:T(8,128)S(1)} %get-tuple-element.66.sin_ref, f32[768,128]{1,0:T(8,128)S(1)} %bitcast.80, f32[8,128]{1,0:T(8,128)S(1)} %get-tuple-element.68.own_ref), custom_call_target="tpu_custom_call" | custom-call | tf_op jit(solution)/shard_map/scan_tiles/pallas_call | solution.py:720
  58.8 18.4 %all_to_all.37 = f32[256,1,128]{2,1,0:T(1,128)S(1)} all-to-all(f32[256,1,128]{2,1,0:T(1,128)S(1)} %bitcast.81), channel_id=1, replica_groups=mesh['tm'=4,'z'=8,'x'=4,'core'=2] {'tm','z','x','core'}, dimensions={0} | all-to-all | bytes 262144 | tf_op jit(solution)/shard_map/all_to_all | solution.py:604
  77.2 1.2 %end_step.1 = (f32[2,4]{1,0:T(2,128)}, f32[2,4]{1,0:T(2,128)}, f32[2,4]{1,0:T(2,128)}, f32[1]{0:T(128)}) custom-call(s32[8,128]{1,0:T(8,128)S(1)} %iota.7.me_ref, f32[256,128]{1,0:T(8,128)S(1)} %bitcast.82, f32[8,128]{1,0:T(8,128)S(1)} %get-tuple-element.68.own_ref), custom_call_target="tpu_custom_call" | custom-call | tf_op jit(solution)/shard_map/end_step/pallas_call | solution.py:734
  (4 shorter events, 0.0 us)
Async XLA Ops:
  22.3 19.9 %copy-start = (f32[48,6,256]{2,0,1:T(8,128)S(1)}, f32[48,6,256]{2,0,1:T(8,128)}, u32[]{:S(2)}) copy-start(f32[48,6,256]{2,0,1:T(8,128)} %param.17) | copy-start | bytes 884740
